TPU v7x, 32 devices: a whole 2x2x4 slice. The times are simulated.
32 devices in a mesh: dp: 8 (over z, x), mp: 4 (over y, core).
Axes of the slice: x: 2, y: 2, z: 4, core: 2. Of those that a mesh axis runs over, the one named last changes fastest.
Arguments:
- hidden_in: bfloat16 [8, 2048, 960], P('dp', 'mp'), may hold values from -6 to 6
- cotangent: bfloat16 [8, 2048, 960], P('dp', 'mp'), may hold values from -6 to 6
- segments: int32 [8, 2048], P('dp'), may hold values from 0 to 3, never falling along the last dimension, each value on 1 to 1024 neighbouring positions
- positions: int32 [8, 2048], P('dp', 'mp'), may hold values from 0 to 4095
- attn_in: bfloat16 [960, 1600], P('dp', 'mp'), may hold values from -0.1875 to 0.1875
- attn_out: bfloat16 [960, 960], P('mp', 'dp'), may hold values from -0.75 to 0.75
- w_gate: bfloat16 [960, 2560], P('dp', 'mp'), may hold values from -0.1875 to 0.1875
- w_up: bfloat16 [960, 2560], P('dp', 'mp'), may hold values from -0.1875 to 0.1875
- w_down: bfloat16 [2560, 960], P('mp', 'dp'), may hold values from -0.125 to 0.125
- norm1_gain: bfloat16 [960], P('dp'), may hold values from 0.099609375 to 1.8984375
- norm2_gain: bfloat16 [960], P('dp'), may hold values from 0.099609375 to 1.8984375
Outputs:
- hidden_out: bfloat16 [8, 2048, 960], P('dp', 'mp')
- grad_hidden: float32 [8, 2048, 960], P('dp', 'mp')
- grad_attn_in: float32 [960, 1600], P('dp', 'mp')
- grad_attn_out: float32 [960, 960], P('mp', 'dp')
- grad_gate: float32 [960, 2560], P('dp', 'mp')
- grad_up: float32 [960, 2560], P('dp', 'mp')
- grad_down: float32 [2560, 960], P('mp', 'dp')
- grad_gain1: float32 [960], P('dp')
- grad_gain2: float32 [960], P('dp')
Inputs may be any that keep to these rules, and one draw needn't show every extreme that they name: `segments`: segment numbers never fall along a sequence; every segment is a run of 1 to 1024 tokens.
All inputs are finite; a program needn't handle non-finite values.
Results may differ from a plain program's by a relative error of at most 0.015.
Values may be sent and summed in bfloat16 or wider, within the bound.
A program may use at most 192 MiB of HBM per device.

v0:
```python
import math

import jax
import jax.numpy as jnp
from jax import lax
from jax.sharding import PartitionSpec as P

HEADS = 15
KV_HEADS = 5
HEAD_DIM = 64


EPSILON = 1e-05
SCORE_SCALE = 0.125
MASK_FILL = -1e30


def rms_forward(values_in, gain):
    inverse = lax.rsqrt(jnp.mean(values_in * values_in, axis=-1, keepdims=True) + EPSILON)
    return (values_in * inverse * gain, inverse)


def rms_backward(values_in, inverse, gain, upstream):
    scaled = upstream * gain
    grad_in = inverse * (
        scaled
        - values_in * inverse * inverse * jnp.mean(scaled * values_in, axis=-1, keepdims=True)
    )
    return (grad_in, jnp.sum(upstream * values_in * inverse, axis=0))


def rotary_tables(position_ids):
    half_dim = HEAD_DIM // 2
    frequency = jnp.exp(
        jnp.arange(half_dim, dtype=jnp.float32) * (-2.0 * math.log(10000.0) / HEAD_DIM)
    )
    angles = position_ids.astype(jnp.float32)[:, None] * frequency[None, :]
    return (jnp.cos(angles)[:, None, :], jnp.sin(angles)[:, None, :])


def rotate(tensor, cosine, sine):
    half_dim = HEAD_DIM // 2
    first, second = (tensor[..., :half_dim], tensor[..., half_dim:])
    return jnp.concatenate(
        [first * cosine - second * sine, second * cosine + first * sine], axis=-1
    )


def rotate_back(tensor, cosine, sine):
    half_dim = HEAD_DIM // 2
    first, second = (tensor[..., :half_dim], tensor[..., half_dim:])
    return jnp.concatenate(
        [first * cosine + second * sine, second * cosine - first * sine], axis=-1
    )


def score_block(queries, keys, allowed):
    scores = (
        jnp.einsum("grd,sd->grs", queries, keys, preferred_element_type=jnp.float32) * SCORE_SCALE
    )
    return jnp.where(allowed[None], scores, MASK_FILL)


def attend(queries, keys, values, allowed):
    scores = score_block(queries, keys, allowed)
    peak = jnp.max(scores, axis=-1, keepdims=True)
    total = jnp.sum(jnp.exp(scores - peak), axis=-1, keepdims=True)
    log_total = peak + jnp.log(total)
    probs = jnp.exp(scores - log_total).astype(jnp.bfloat16)
    output = jnp.einsum("grs,sd->grd", probs, values, preferred_element_type=jnp.float32)
    return (output, log_total[..., 0])


def attend_back(queries, keys, values, allowed, log_total, output_b, grad_out_b):
    scores = score_block(queries, keys, allowed)
    probs = jnp.exp(scores - log_total[..., None])
    probs_b = probs.astype(jnp.bfloat16)
    grad_probs = jnp.einsum("grd,sd->grs", grad_out_b, values, preferred_element_type=jnp.float32)
    delta = jnp.sum(
        grad_out_b.astype(jnp.float32) * output_b.astype(jnp.float32), axis=-1, keepdims=True
    )
    grad_scores = (probs * (grad_probs - delta)).astype(jnp.bfloat16)
    grad_q = (
        jnp.einsum("grs,sd->grd", grad_scores, keys, preferred_element_type=jnp.float32)
        * SCORE_SCALE
    )
    grad_k = (
        jnp.einsum("grs,grd->sd", grad_scores, queries, preferred_element_type=jnp.float32)
        * SCORE_SCALE
    )
    grad_v = jnp.einsum("grs,grd->sd", probs_b, grad_out_b, preferred_element_type=jnp.float32)
    return (grad_q, grad_k, grad_v)


def per_device(
    hidden_in,
    cotangent,
    segments,
    positions,
    attn_in,
    attn_out,
    w_gate,
    w_up,
    w_down,
    norm1_gain,
    norm2_gain,
):
    tok_rows = hidden_in.shape[1]
    model_size = lax.axis_size("mp")
    seq_rows = tok_rows * model_size
    model_rank = lax.axis_index("mp")
    group_size = HEADS // KV_HEADS
    query_cols = HEADS * HEAD_DIM
    kv_cols = KV_HEADS * HEAD_DIM
    gathered = (
        lax.all_gather(attn_in, "dp", axis=0, tiled=True),
        lax.all_gather(attn_out, "dp", axis=1, tiled=True),
        lax.all_gather(w_gate, "dp", axis=0, tiled=True),
        lax.all_gather(w_up, "dp", axis=0, tiled=True),
        lax.all_gather(w_down, "dp", axis=1, tiled=True),
        lax.all_gather(norm1_gain, "dp", axis=0, tiled=True),
        lax.all_gather(norm2_gain, "dp", axis=0, tiled=True),
    )
    qkv_weight, out_weight = (
        lax.all_gather(gathered[0], "mp", axis=1, tiled=True),
        lax.all_gather(gathered[1], "mp", axis=0, tiled=True),
    )
    gate_weight, up_weight, down_weight = (gathered[2], gathered[3], gathered[4])
    gain_one = gathered[5].astype(jnp.float32)
    gain_two = gathered[6].astype(jnp.float32)
    resid_in = hidden_in[0].astype(jnp.float32)
    normed1, inv_one = rms_forward(resid_in, gain_one)
    normed1_b = normed1.astype(jnp.bfloat16)
    projected = jnp.dot(normed1_b, qkv_weight, preferred_element_type=jnp.float32)
    cosine, sine = rotary_tables(positions[0])
    queries = rotate(
        projected[:, :query_cols].reshape(tok_rows, HEADS, HEAD_DIM), cosine, sine
    ).astype(jnp.bfloat16)
    keys_own = (
        rotate(
            projected[:, query_cols : query_cols + kv_cols].reshape(tok_rows, KV_HEADS, HEAD_DIM),
            cosine,
            sine,
        )
        .astype(jnp.bfloat16)
        .reshape(tok_rows, kv_cols)
    )
    values_own = projected[:, query_cols + kv_cols :].astype(jnp.bfloat16)
    keys_all, values_all = (
        lax.all_gather(keys_own, "mp", axis=0, tiled=True),
        lax.all_gather(values_own, "mp", axis=0, tiled=True),
    )
    seq_seg = segments[0]
    query_seg = lax.dynamic_slice_in_dim(seq_seg, model_rank * tok_rows, tok_rows, 0)
    query_index = model_rank * tok_rows + jnp.arange(tok_rows, dtype=jnp.int32)
    key_index = jnp.arange(seq_rows, dtype=jnp.int32)
    allowed = (query_seg[:, None] == seq_seg[None, :]) & (
        key_index[None, :] <= query_index[:, None]
    )
    query_groups = queries.reshape(tok_rows, KV_HEADS, group_size, HEAD_DIM).transpose(1, 2, 0, 3)
    key_groups = keys_all.reshape(seq_rows, KV_HEADS, HEAD_DIM).transpose(1, 0, 2)
    value_groups = values_all.reshape(seq_rows, KV_HEADS, HEAD_DIM).transpose(1, 0, 2)
    outputs, log_totals = lax.map(
        lambda pack: attend(pack[0], pack[1], pack[2], allowed),
        (query_groups, key_groups, value_groups),
    )
    out_groups = outputs.astype(jnp.bfloat16)
    attn_b = out_groups.transpose(2, 0, 1, 3).reshape(tok_rows, query_cols)
    middle = resid_in + jnp.dot(attn_b, out_weight, preferred_element_type=jnp.float32)
    normed2, inv_two = rms_forward(middle, gain_two)
    normed2_b = normed2.astype(jnp.bfloat16)
    seq_normed = lax.all_gather(normed2_b, "mp", axis=0, tiled=True)
    gate = jnp.dot(seq_normed, gate_weight, preferred_element_type=jnp.float32)
    upper = jnp.dot(seq_normed, up_weight, preferred_element_type=jnp.float32)
    sigma = jax.nn.sigmoid(gate)
    silu_gate = gate * sigma
    hidden_b = (silu_gate * upper).astype(jnp.bfloat16)
    ffn_out = lax.psum_scatter(
        jnp.dot(hidden_b, down_weight, preferred_element_type=jnp.float32).astype(jnp.bfloat16),
        "mp",
        scatter_dimension=0,
        tiled=True,
    ).astype(jnp.float32)
    hidden_out = (middle + ffn_out).astype(jnp.bfloat16)
    regathered = (
        lax.all_gather(attn_in, "dp", axis=0, tiled=True),
        lax.all_gather(attn_out, "dp", axis=1, tiled=True),
        lax.all_gather(w_gate, "dp", axis=0, tiled=True),
        lax.all_gather(w_up, "dp", axis=0, tiled=True),
        lax.all_gather(w_down, "dp", axis=1, tiled=True),
        lax.all_gather(norm1_gain, "dp", axis=0, tiled=True),
        lax.all_gather(norm2_gain, "dp", axis=0, tiled=True),
    )
    qkv_weight, out_weight = (
        lax.all_gather(regathered[0], "mp", axis=1, tiled=True),
        lax.all_gather(regathered[1], "mp", axis=0, tiled=True),
    )
    gate_weight, up_weight, down_weight = (regathered[2], regathered[3], regathered[4])
    gain_one = regathered[5].astype(jnp.float32)
    gain_two = regathered[6].astype(jnp.float32)
    cot_local = cotangent[0]
    seq_cot = lax.all_gather(cot_local, "mp", axis=0, tiled=True)
    g_down = jnp.dot(hidden_b.T, seq_cot, preferred_element_type=jnp.float32)
    grad_hid = jnp.dot(seq_cot, down_weight.T, preferred_element_type=jnp.float32)
    grad_gate_act = (grad_hid * upper * sigma * (1.0 + gate * (1.0 - sigma))).astype(jnp.bfloat16)
    grad_up_act = (grad_hid * silu_gate).astype(jnp.bfloat16)
    g_gate = jnp.dot(seq_normed.T, grad_gate_act, preferred_element_type=jnp.float32)
    g_up = jnp.dot(seq_normed.T, grad_up_act, preferred_element_type=jnp.float32)
    grad_norm2 = lax.psum_scatter(
        jnp.dot(grad_gate_act, gate_weight.T, preferred_element_type=jnp.float32)
        + jnp.dot(grad_up_act, up_weight.T, preferred_element_type=jnp.float32),
        "mp",
        scatter_dimension=0,
        tiled=True,
    )
    grad_mid_norm, g_gain2 = rms_backward(middle, inv_two, gain_two, grad_norm2)
    grad_middle = cot_local.astype(jnp.float32) + grad_mid_norm
    middle_b = grad_middle.astype(jnp.bfloat16)
    g_out = jnp.dot(attn_b.T, middle_b, preferred_element_type=jnp.float32)
    grad_attn_b = jnp.dot(middle_b, out_weight.T, preferred_element_type=jnp.float32).astype(
        jnp.bfloat16
    )
    grad_groups = grad_attn_b.reshape(tok_rows, KV_HEADS, group_size, HEAD_DIM).transpose(
        1, 2, 0, 3
    )
    grad_q, grad_k, grad_v = lax.map(
        lambda pack: attend_back(pack[0], pack[1], pack[2], allowed, pack[3], pack[4], pack[5]),
        (query_groups, key_groups, value_groups, log_totals, out_groups, grad_groups),
    )
    key_grads, value_grads = (
        lax.psum_scatter(grad_k, "mp", scatter_dimension=1, tiled=True),
        lax.psum_scatter(grad_v, "mp", scatter_dimension=1, tiled=True),
    )
    grad_q = rotate_back(
        grad_q.transpose(2, 0, 1, 3).reshape(tok_rows, HEADS, HEAD_DIM), cosine, sine
    )
    key_grads = rotate_back(key_grads.transpose(1, 0, 2), cosine, sine)
    value_grads = value_grads.transpose(1, 0, 2)
    grad_proj = jnp.concatenate(
        [
            grad_q.reshape(tok_rows, query_cols),
            key_grads.reshape(tok_rows, kv_cols),
            value_grads.reshape(tok_rows, kv_cols),
        ],
        axis=1,
    ).astype(jnp.bfloat16)
    g_in = jnp.dot(normed1_b.T, grad_proj, preferred_element_type=jnp.float32)
    grad_norm1 = jnp.dot(grad_proj, qkv_weight.T, preferred_element_type=jnp.float32)
    grad_in_norm, g_gain1 = rms_backward(resid_in, inv_one, gain_one, grad_norm1)
    grad_input = grad_middle + grad_in_norm
    reduced = (
        lax.psum_scatter(g_in, "dp", scatter_dimension=0, tiled=True),
        lax.psum_scatter(g_out, "dp", scatter_dimension=1, tiled=True),
        lax.psum_scatter(g_gate, "dp", scatter_dimension=0, tiled=True),
        lax.psum_scatter(g_up, "dp", scatter_dimension=0, tiled=True),
        lax.psum_scatter(g_down, "dp", scatter_dimension=1, tiled=True),
        lax.psum_scatter(g_gain1, "dp", scatter_dimension=0, tiled=True),
        lax.psum_scatter(g_gain2, "dp", scatter_dimension=0, tiled=True),
    )
    grad_attn_in, grad_attn_out = (
        lax.psum_scatter(reduced[0], "mp", scatter_dimension=1, tiled=True),
        lax.psum_scatter(reduced[1], "mp", scatter_dimension=0, tiled=True),
    )
    grad_gain1, grad_gain2 = lax.psum((reduced[5], reduced[6]), "mp")
    return (
        hidden_out[None],
        grad_input[None],
        grad_attn_in,
        grad_attn_out,
        reduced[2],
        reduced[3],
        reduced[4],
        grad_gain1,
        grad_gain2,
    )


def solution(mesh):
    return jax.shard_map(
        per_device,
        mesh=mesh,
        in_specs=(
            P("dp", "mp", None),
            P("dp", "mp", None),
            P("dp", None),
            P("dp", "mp"),
            P("dp", "mp"),
            P("mp", "dp"),
            P("dp", "mp"),
            P("dp", "mp"),
            P("mp", "dp"),
            P("dp"),
            P("dp"),
        ),
        out_specs=(
            P("dp", "mp", None),
            P("dp", "mp", None),
            P("dp", "mp"),
            P("mp", "dp"),
            P("dp", "mp"),
            P("dp", "mp"),
            P("mp", "dp"),
            P("dp"),
            P("dp"),
        ),
        check_vma=False,
    )
```

profile of v0, /device:TPU:0, one launch (start us, length us, event | category | flops | bytes accessed | tf_op | source)
XLA Modules:
  0.0 1195.8 jit_solution(7193035129277229926)
XLA Ops:
  7.3 34.3 %all-gather.1 = bf16[8,120,400]{1,2,0:T(8,128)(2,1)S(1)} all-gather(bf16[1,120,400]{1,2,0:T(8,128)(2,1)} %bitcast.241), channel_id=1, replica_groups=mesh['dp'=8,'mp'=4] {'dp'}, dimensions={0}, use_global_device_ids=true | all-gather | bytes 864000 | tf_op jit(solution)/shard_map/all_gather | solution.py:116
  45.2 21.3 %all-reduce.10 = (bf16[960]{0:T(1024)(128)(2,1)S(1)}, bf16[960]{0:T(1024)(128)(2,1)S(1)}) all-reduce(bf16[960]{0:T(1024)(128)(2,1)S(1)} %dynamic-update-slice, bf16[960]{0:T(1024)(128)(2,1)S(1)} %dynamic-update-slice.1), channel_id=1, replica_groups=mesh['dp'=8,'mp'=4] {'dp'}, use_global_device_ids=true, to_apply=%add | all-reduce | flops 1920 | bytes 7680
  80.2 33.2 %all_gather.53 = bf16[240,960]{0,1:T(8,128)(2,1)} all-gather(bf16[240,120]{0,1:T(8,128)(2,1)S(1)} %copy.27), channel_id=1, replica_groups=mesh['dp'=8,'mp'=4] {'dp'}, dimensions={1}, use_global_device_ids=true | all-gather | bytes 518400 | tf_op jit(solution)/shard_map/all_gather | solution.py:117
  117.5 114.8 %while.30 = (s32[]{:T(128)}, bf16[5,3,512,64]{2,3,1,0:T(8,128)(2,1)S(1)}, f32[5,3,512]{2,1,0:T(4,128)S(1)}, bf16[5,3,512,64]{2,3,1,0:T(8,128)(2,1)S(1)}, bf16[5,...) while((s32[]{:T(128)}, ...), condition=%wide.region_4.5_spmd.clone.clone, body=%wide.region_1.4_spmd.clone.sunk.clone | while | flops 843053568 | bytes 43130984 | solution.py:163
  132.8 8.1 fusion.160
  155.8 8.1 fusion.160
  178.6 8.0 fusion.160
  201.5 8.0 fusion.160
  224.3 8.0 fusion.160
  240.1 30.8 %all-gather.20.cloned.1.call-done = bf16[2048,960]{0,1:T(8,128)(2,1)} async-done(((bf16[512,960]{0,1:T(8,128)(2,1)}), bf16[2048,960]{0,1:T(8,128)(2,1)}) %all-gather.20.cloned.1.call-update) | async-done | bytes 3932176 | tf_op jit(solution)/shard_map/all_gather | solution.py:172
  270.9 8.3 fusion.89
  279.2 35.4 %all-gather.22.cloned.1.call-done = bf16[960,640]{1,0:T(8,128)(2,1)} async-done(((bf16[120,640]{1,0:T(8,128)(2,1)}), bf16[960,640]{1,0:T(8,128)(2,1)}) %all-gather.22.cloned.1.call-update) | async-done | bytes 1228816 | tf_op jit(solution)/shard_map/all_gather | solution.py:118
  314.6 8.3 fusion.88
  322.9 34.1 %all-gather.26.cloned.1.call-done = bf16[640,960]{0,1:T(8,128)(2,1)} async-done(((bf16[640,120]{0,1:T(8,128)(2,1)}), bf16[640,960]{0,1:T(8,128)(2,1)}) %all-gather.26.cloned.1.call-update) | async-done | bytes 1228816 | tf_op jit(solution)/shard_map/all_gather | solution.py:120
  357.0 33.4 %all-gather.28.cloned.1.call-done = bf16[1,2048,960]{1,2,0:T(8,128)(2,1)} async-done(((bf16[1,512,960]{1,2,0:T(8,128)(2,1)}), bf16[1,2048,960]{1,2,0:T(8,128)(2,1)}) %all-gather.28.cloned.1.call-update) | async-done | bytes 3932176 | tf_op jit(solution)/shard_map/all_gather | solution.py:202
  390.4 12.7 %multiply_convert_fusion.1 = (bf16[2048,640]{1,0:T(8,128)(2,1)S(1)}, bf16[2048,640]{1,0:T(8,128)(2,1)S(1)}, bf16[2048,640]{1,0:T(8,128)(2,1)}) fusion(f32[2048,640]{1,0:T(8,128)} %fusion.88, f32[2048,640]{1,0:T(8,128)} %fusion.89, bf16[640,960]{0,1:T(8,128)(2,1)} %all-gather.26.cloned.1.call-done, bf16[1,2048,960]{1,2,0:T(8,128)(2,1)} %all-gather.28.cloned.1.call-done), kind=kOutput, calls=%fused_computation.66 | convolution fusion | flops 2536243200 | bytes 23511040 | tf_op jit(solution)/shard_map/dot_general | solution.py:204
  419.3 61.8 %reduce-scatter.26.cloned.1.call-done = f32[512,960]{0,1:T(8,128)} async-done(((f32[2048,960]{0,1:T(8,128)}), f32[512,960]{0,1:T(8,128)}) %reduce-scatter.26.cloned.1.call-update) | async-done | bytes 1966096 | tf_op jit(solution)/shard_map/reduce_scatter | solution.py:209
  483.8 42.9 %reduce-scatter.24.cloned.1.call-done = bf16[512,960]{0,1:T(8,128)(2,1)} async-done(((bf16[2048,960]{0,1:T(8,128)(2,1)}), bf16[512,960]{0,1:T(8,128)(2,1)}) %reduce-scatter.24.cloned.1.call-update) | async-done | bytes 983056 | tf_op jit(solution)/shard_map/reduce_scatter | solution.py:178
  531.9 101.6 %while.31 = (s32[]{:T(128)}, f32[5,3,512,64]{2,3,1,0:T(8,128)}, f32[5,2048,64]{1,2,0:T(8,128)}, f32[5,2048,64]{1,2,0:T(8,128)}, bf16[5,3,512,64]{2,3,1,0:T(8,128...) while((s32[]{:T(128)}, f32[5,3,512,64]{2,3,1,0:T(8,128)}, ...), condition=%wide.region_11.12_spmd.clone.clone, body=%wide.region_9.11_spmd.clone.sunk.clone | while | flops 2048489984 | bytes 63237260 | solution.py:226
  641.9 26.4 %reduce-scatter.30.cloned.1.call-done = f32[5,512,64]{1,2,0:T(8,128)} async-done(((f32[5,2048,64]{1,2,0:T(8,128)}), f32[5,512,64]{1,2,0:T(8,128)}) %reduce-scatter.30.cloned.1.call-update) | async-done | bytes 655376 | tf_op jit(solution)/shard_map/reduce_scatter | solution.py:232
  670.2 35.5 %reduce-scatter.28.cloned.1.call-done = f32[5,512,64]{1,2,0:T(8,128)} async-done(((f32[5,2048,64]{1,2,0:T(8,128)}), f32[5,512,64]{1,2,0:T(8,128)}) %reduce-scatter.28.cloned.1.call-update) | async-done | bytes 655376 | tf_op jit(solution)/shard_map/reduce_scatter | solution.py:231
  713.0 7.6 fusion.61
  720.7 7.6 fusion.91
  728.4 7.7 fusion.92
  736.1 57.5 %reduce-scatter.36.cloned.1.call-done = f32[120,960]{1,0:T(8,128)} async-done(((f32[960,960]{1,0:T(8,128)}), f32[120,960]{1,0:T(8,128)}) %reduce-scatter.36.cloned.1.call-update) | async-done | bytes 460816
  796.0 122.4 %reduce-scatter.38.cloned.1.call-done = f32[120,1600]{1,0:T(8,128)} async-done(((f32[960,1600]{1,0:T(8,128)}), f32[120,1600]{1,0:T(8,128)}) %reduce-scatter.38.cloned.1.call-update) | async-done | bytes 768016
  927.2 20.1 %all-reduce.8 = (f32[960]{0:T(1024)S(1)}, f32[960]{0:T(1024)S(1)}) all-reduce(f32[960]{0:T(1024)S(1)} %get-tuple-element.203, f32[960]{0:T(1024)S(1)} %copy-done.14), channel_id=14, replica_groups=mesh['dp'=8,'mp'=4] {'dp'}, use_global_device_ids=true, to_apply=%region_23.24.clone | all-reduce | flops 1920 | bytes 15360
  957.3 34.7 %reduce-scatter.44.cloned.1.call-done = f32[640,120]{0,1:T(8,128)} async-done(((f32[640,960]{0,1:T(8,128)}), f32[640,120]{0,1:T(8,128)}) %reduce-scatter.44.cloned.1.call-update) | async-done | bytes 307216
  992.0 73.3 %reduce-scatter.40.cloned.1.call-done = f32[120,640]{1,0:T(8,128)} async-done(((f32[960,640]{1,0:T(8,128)}), f32[120,640]{1,0:T(8,128)}) %reduce-scatter.40.cloned.1.call-update) | async-done | bytes 307216
  1065.3 73.2 %reduce-scatter.42.cloned.1.call-done = f32[120,640]{1,0:T(8,128)} async-done(((f32[960,640]{1,0:T(8,128)}), f32[120,640]{1,0:T(8,128)}) %reduce-scatter.42.cloned.1.call-update) | async-done | bytes 307216
  1138.5 23.6 %reduce-scatter.32.cloned.1.call-done = f32[240,120]{1,0:T(8,128)} async-done(((f32[960,120]{1,0:T(8,128)}), f32[240,120]{1,0:T(8,128)}) %reduce-scatter.32.cloned.1.call-update) | async-done | bytes 115216 | tf_op jit(solution)/shard_map/reduce_scatter | solution.py:262
  1162.1 26.6 %reduce-scatter.34.cloned.1.call-done = f32[400,120]{1,0:T(8,128)} async-done(((f32[1600,120]{1,0:T(8,128)}), f32[400,120]{1,0:T(8,128)}) %reduce-scatter.34.cloned.1.call-update) | async-done | bytes 192016
  (214 shorter events, 265.9 us)
Async XLA Ops:
  7.2 36.2 %copy-start.19 = (u32[32]{0:T(128)S(1)}, u32[32]{0:T(128)}, u32[]{:S(2)}) copy-start(u32[32]{0:T(128)} %constant.80) | copy-start | bytes 388
  7.2 37.6 %copy-start.23 = (bf16[120]{0:T(256)(128)(2,1)S(1)}, bf16[120]{0:T(256)(128)(2,1)}, u32[]{:S(2)}) copy-start(bf16[120]{0:T(256)(128)(2,1)} %param.24) | copy-start | bytes 724
  7.2 37.8 %copy-start.24 = (bf16[120]{0:T(256)(128)(2,1)S(1)}, bf16[120]{0:T(256)(128)(2,1)}, u32[]{:S(2)}) copy-start(bf16[120]{0:T(256)(128)(2,1)} %param.25) | copy-start | bytes 724
  7.2 59.3 %copy-start.5 = (bf16[1,512,960]{1,2,0:T(8,128)(2,1)S(1)}, bf16[1,512,960]{1,2,0:T(8,128)(2,1)}, u32[]{:S(2)}) copy-start(bf16[1,512,960]{1,2,0:T(8,128)(2,1)} %param.15) | copy-start | bytes 2949124
  7.2 66.5 %all-gather.12.cloned.1.call-start = ((), (), s32[]{:S(2)}) async-start(), calls=%async_computation.11 | async-start | bytes 4096000 | tf_op jit(solution)/shard_map/all_gather | solution.py:125
  43.4 74.1 %all-gather.16.cloned.1.call-start = ((), (), s32[]{:S(2)}) async-start(), calls=%async_computation.13 | async-start | bytes 1638400 | tf_op jit(solution)/shard_map/all_gather | solution.py:151
  77.8 37.6 %copy-start.3 = (f32[512,1600]{0,1:T(8,128)}, f32[512,1600]{0,1:T(8,128)S(1)}, u32[]{:S(2)}) copy-start(f32[512,1600]{0,1:T(8,128)S(1)} %fusion.83) | copy-start | bytes 9830404
  78.7 38.8 %all-gather.14.cloned.1.call-start = ((), (), s32[]{:S(2)}) async-start(), calls=%async_computation.12 | async-start | bytes 1638400 | tf_op jit(solution)/shard_map/all_gather | solution.py:150
  79.1 37.4 %copy-start.7 = (f32[512,32]{0,1:T(8,128)}, f32[512,32]{0,1:T(8,128)S(1)}, u32[]{:S(2)}) copy-start(f32[512,32]{0,1:T(8,128)S(1)} %get-tuple-element.272) | copy-start | bytes 196612
  79.1 37.4 %copy-start.9 = (f32[512,32]{0,1:T(8,128)}, f32[512,32]{0,1:T(8,128)S(1)}, u32[]{:S(2)}) copy-start(f32[512,32]{0,1:T(8,128)S(1)} %get-tuple-element.273) | copy-start | bytes 196612
  79.2 37.3 %copy-start.12 = (s32[1,2048]{1,0:T(1,128)S(1)}, s32[1,2048]{1,0:T(1,128)}, u32[]{:S(2)}) copy-start(s32[1,2048]{1,0:T(1,128)} %param.17) | copy-start | bytes 24580
  80.1 152.3 %all-gather.18.cloned.1.call-start = ((), (), s32[]{:S(2)}) async-start(), calls=%async_computation.14 | async-start | bytes 2457600 | tf_op jit(solution)/shard_map/all_gather | solution.py:126
  115.5 124.6 %all-gather.24.cloned.1.call-start = ((), (), s32[]{:S(2)}) async-start(), calls=%async_computation.17 | async-start | bytes 1382400 | tf_op jit(solution)/shard_map/all_gather | solution.py:119
  116.1 154.8 %all-gather.20.cloned.1.call-start = ((), (), s32[]{:S(2)}) async-start(), calls=%async_computation.15 | async-start | bytes 4915200 | tf_op jit(solution)/shard_map/all_gather | solution.py:172
  237.5 77.0 %all-gather.22.cloned.1.call-start = ((), (), s32[]{:S(2)}) async-start(), calls=%async_computation.16 | async-start | bytes 1382400 | tf_op jit(solution)/shard_map/all_gather | solution.py:118
  238.3 118.7 %all-gather.26.cloned.1.call-start = ((), (), s32[]{:S(2)}) async-start(), calls=%async_computation.18 | async-start | bytes 1382400 | tf_op jit(solution)/shard_map/all_gather | solution.py:120
  239.1 151.4 %all-gather.28.cloned.1.call-start = ((), (), s32[]{:S(2)}) async-start(), calls=%async_computation.24 | async-start | bytes 4915200 | tf_op jit(solution)/shard_map/all_gather | solution.py:202
  239.8 241.3 %reduce-scatter.26.cloned.1.call-start = ((), (), s32[]{:S(2)}) async-start(), calls=%async_computation.20 | async-start | bytes 9830400 | tf_op jit(solution)/shard_map/reduce_scatter | solution.py:209
  390.4 12.8 %copy-start.22 = (bf16[960,640]{1,0:T(8,128)(2,1)S(1)}, bf16[960,640]{1,0:T(8,128)(2,1)}, u32[]{:S(2)}) copy-start(bf16[960,640]{1,0:T(8,128)(2,1)} %all-gather.22.cloned.1.call-done) | copy-start | bytes 3686404
  412.0 114.8 %reduce-scatter.24.cloned.1.call-start = ((), (), s32[]{:S(2)}) async-start(), calls=%async_computation.19 | async-start | bytes 4915200 | tf_op jit(solution)/shard_map/reduce_scatter | solution.py:178
  419.2 249.1 %reduce-scatter.30.cloned.1.call-start = ((), (), s32[]{:S(2)}) async-start(), calls=%async_computation.22 | async-start | bytes 3276800 | tf_op jit(solution)/shard_map/reduce_scatter | solution.py:232
  633.5 72.2 %reduce-scatter.28.cloned.1.call-start = ((), (), s32[]{:S(2)}) async-start(), calls=%async_computation.21 | async-start | bytes 3276800 | tf_op jit(solution)/shard_map/reduce_scatter | solution.py:231
  634.2 159.4 %reduce-scatter.36.cloned.1.call-start = ((), (), s32[]{:S(2)}) async-start(), calls=%async_computation.26 | async-start | bytes 4423680
  638.2 280.3 %reduce-scatter.38.cloned.1.call-start = ((), (), s32[]{:S(2)}) async-start(), calls=%async_computation.27 | async-start | bytes 7188480
  640.9 66.1 %copy-start.6 = (bf16[1,512,960]{1,2,0:T(8,128)(2,1)S(1)}, bf16[1,512,960]{1,2,0:T(8,128)(2,1)}, u32[]{:S(2)}) copy-start(bf16[1,512,960]{1,2,0:T(8,128)(2,1)} %param.15) | copy-start | bytes 2949124
  640.9 66.1 %copy-start.16 = (f32[960]{0:T(1024)S(1)}, f32[960]{0:T(1024)}, u32[]{:S(2)}) copy-start(f32[960]{0:T(1024)} %copy-done.15) | copy-start | bytes 11524
  640.9 66.1 %copy-start.18 = (f32[512]{0:T(512)S(1)}, f32[512]{0:T(512)}, u32[]{:S(2)}) copy-start(f32[512]{0:T(512)} %copy-done.17) | copy-start | bytes 6148
  713.0 279.0 %reduce-scatter.44.cloned.1.call-start = ((), (), s32[]{:S(2)}) async-start(), calls=%async_computation.30 | async-start | bytes 2764800
  720.6 344.7 %reduce-scatter.40.cloned.1.call-start = ((), (), s32[]{:S(2)}) async-start(), calls=%async_computation.28 | async-start | bytes 2764800
  728.3 410.2 %reduce-scatter.42.cloned.1.call-start = ((), (), s32[]{:S(2)}) async-start(), calls=%async_computation.29 | async-start | bytes 2764800
  736.0 426.0 %reduce-scatter.32.cloned.1.call-start = ((), (), s32[]{:S(2)}) async-start(), calls=%async_computation.23 | async-start | bytes 614400 | tf_op jit(solution)/shard_map/reduce_scatter | solution.py:262
  795.7 393.0 %reduce-scatter.34.cloned.1.call-start = ((), (), s32[]{:S(2)}) async-start(), calls=%async_computation.25 | async-start | bytes 1024000
  (15 other events, 63.1 us)
Sparse Core Ops, SparseCore 0:
  43.5 30.1 all-gather.11
  78.8 18.1 all-gather.15
  99.2 18.1 all-gather.13
  119.4 21.8 all-gather.17
  143.3 41.4 all-gather.23
  237.7 33.2 all-gather.19
  273.1 41.4 all-gather.21
  316.8 40.2 all-gather.25
  358.6 31.7 all-gather.27
  412.1 68.9 reduce-scatter.25
  483.8 42.8 reduce-scatter.23
  633.6 34.6 reduce-scatter.29
  671.0 34.6 reduce-scatter.27
  709.3 84.3 reduce-scatter.35
  797.5 120.8 reduce-scatter.37
  922.9 69.0 reduce-scatter.43
  996.5 68.8 reduce-scatter.39
  1069.8 68.6 reduce-scatter.41
  1141.7 20.2 reduce-scatter.31
  1165.2 23.4 reduce-scatter.33
where the time goes:
time: 1200 us
  waiting for transfers between devices  722 us (60%)
  matrix products  261 us (22%)
  blocking collectives  115 us (10%)
  other arithmetic  65.6 us (5%)
  between operations  16.4 us (1%)
  local copies, waits for them, and re-layouts  13.4 us (1%)
    unnamed x26, waiting for transfers between devices  391 us
    reduce_scatter x1, waiting for transfers between devices, per_device(): lax.psum_scatter(jnp.dot(grad_gate_act, gate_weight.T, preferred_element_...  61.8 us
    dot_general x10, matrix products, score_block(): jnp.einsum('grd,sd->grs', queries, keys, preferred_element_type=jnp.float32)  48.5 us
    reduce_scatter x1, waiting for transfers between devices, per_device(): lax.psum_scatter(jnp.dot(hidden_b, down_weight, preferred_element_type=jn...  42.9 us
    unnamed x2, blocking collectives  41.4 us
    dot_general x5, matrix products, attend(): jnp.einsum('grs,sd->grd', probs, values, preferred_element_type=jnp.float32)  40.2 us
    reduce_scatter x1, waiting for transfers between devices, per_device(): lax.psum_scatter(grad_k, 'mp', scatter_dimension=1, tiled=True)  35.5 us
    all_gather x1, waiting for transfers between devices, per_device(): lax.all_gather(w_gate, 'dp', axis=0, tiled=True)  35.4 us
  transfers between devices with their start and end apart: 20, of which 16 were waited for; matrix products, arithmetic and copies ran while one was open for 17% of the time, Pallas kernels for 0%

commit v1 on v0

v1 whole, which is shorter than its diff:
```python
import functools
import math

import jax
import jax.numpy as jnp
from jax import lax
from jax.experimental import pallas as pl
from jax.experimental.pallas import tpu as pltpu
from jax.sharding import PartitionSpec as P

HEADS = 15
KV_HEADS = 5
GROUP = HEADS // KV_HEADS
HEAD_DIM = 64
DPAD = 1024
TILE = 256
EPSILON = 1e-05
SCORE_SCALE = 0.125
MASK_FILL = -1e30
LOG2E = 1.4426950408889634
EXP_SCALE = SCORE_SCALE * LOG2E
BF16 = jnp.bfloat16
F32 = jnp.float32


def dot(a, b):
    return jnp.dot(a, b, preferred_element_type=F32)


def dot_nt(a, b):
    return lax.dot_general(a, b, (((1,), (1,)), ((), ())), preferred_element_type=F32)


def vmem_specs(count):
    return [pl.BlockSpec(memory_space=pltpu.VMEM)] * count


def params():
    return pltpu.CompilerParams(vmem_limit_bytes=56 << 20)


class Links:
    def __init__(self, dp_size):
        self.dp_size = dp_size
        self.depth = dp_size // 2

    def pairs(self, move):
        found = []
        for d in range(self.dp_size):
            for m in range(4):
                target = move(d, m)
                if target is not None:
                    found.append((d * 4 + m, target[0] * 4 + target[1]))
        return found

    def send(self, value, move):
        return lax.ppermute(value, ("dp", "mp"), self.pairs(move))

    def over_z(self, value, k):
        return self.send(value, lambda d, m: (d ^ (2 * k), m))

    def over_x(self, value):
        return self.send(value, lambda d, m: (d ^ 1, m))

    def over_y(self, value):
        return self.send(value, lambda d, m: (d, m ^ 2))

    def over_core(self, value):
        return self.send(value, lambda d, m: (d, m ^ 1))

    def some(self, value, table):
        return self.send(value, lambda d, m: (d, table[m]) if m in table else None)

    def gather(self, value):
        half = self.depth // 2
        own = jnp.stack([value] + [self.over_z(value, k) for k in range(1, self.depth)])
        by_x = self.over_x(own)
        by_y = self.over_y(own)
        low = self.over_y(by_x[:half])
        high = self.over_x(by_y[half:])
        return own, by_x, by_y, low, high

    def scatter(self, parts):
        p00, p01a, p01b, p10a, p10b, p11a, p11b = parts
        half = self.depth // 2
        r11a = self.over_y(p11a)
        r11b = self.over_x(p11b)
        r01b = self.over_x(p01b)
        r10a = self.over_y(p10a)
        s01a = (p01a.astype(F32) + r11a.astype(F32)).astype(BF16)
        s10b = (p10b.astype(F32) + r11b.astype(F32)).astype(BF16)
        r01a = self.over_x(s01a)
        r10b = self.over_y(s10b)
        sums = p00.astype(F32) + jnp.concatenate(
            [r10a.astype(F32) + r01a.astype(F32), r01b.astype(F32) + r10b.astype(F32)], axis=0
        )
        total = sums[0]
        for k in range(1, self.depth):
            total = total + self.over_z(sums[k].astype(BF16), k).astype(F32)
        return total

    def all_sum(self, value):
        value = value + self.over_core(value)
        value = value + self.over_y(value)
        value = value + self.over_x(value)
        k = 1
        while k < self.depth:
            value = value + self.over_z(value, k)
            k *= 2
        return value


def assemble_kernel(depth, rows, pad, ids, own, by_x, by_y, low, high, out):
    dp_index, y = ids[0], ids[1]
    half = depth // 2
    out[...] = jnp.zeros_like(out)
    for jz in range(depth):
        for jx in range(2):
            for jy in range(2):
                if jx and jy:
                    block = low[jz] if jz < half else high[jz - half]
                else:
                    block = (by_x if jx else by_y if jy else own)[jz]
                start = pl.multiple_of((dp_index ^ (2 * jz + jx)) * pad, pad)
                out[y ^ jy, pl.ds(start, rows), :] = block


def assemble(blocks, ids):
    depth, rows, cols = blocks[0].shape
    pad = DPAD // (2 * depth)
    return pl.pallas_call(
        functools.partial(assemble_kernel, depth, rows, pad),
        out_shape=jax.ShapeDtypeStruct((2, DPAD, cols), BF16),
        in_specs=[pl.BlockSpec(memory_space=pltpu.SMEM)] + vmem_specs(5),
        out_specs=pl.BlockSpec(memory_space=pltpu.VMEM),
        compiler_params=params(),
        cost_estimate=pl.CostEstimate(
            flops=0, bytes_accessed=DPAD * cols * 8, transcendentals=0
        ),
        name="assemble",
    )(ids, *blocks)


def wgrad_plane_kernel(depth, rows, pad, ids, lhs, rhs, *refs):
    outs, acc = refs[:-1], refs[-1]
    dp_index, y = ids[0], ids[1]
    z, x = dp_index // 2, dp_index % 2
    half = depth // 2
    for part in range(2):

        def body(i, carry):
            jz = part * half + i
            start = pl.multiple_of((z ^ jz) * (2 * pad), 2 * pad)
            left = lhs[pl.ds(start, 2 * pad), :]
            for jy in range(2):
                acc[...] = dot(left, rhs[y ^ jy])
                for jx in range(2):
                    block = acc[pl.ds(pl.multiple_of((x ^ jx) * pad, pad), rows), :]
                    if jy == 0 and jx == 0:
                        outs[0][jz] = block.astype(BF16)
                    else:
                        outs[1 + 2 * (2 * jy + jx - 1) + part][i] = block.astype(BF16)
            return carry

        lax.fori_loop(0, half, body, 0)


def wgrad_plane(lhs, rhs, ids, depth, rows):
    pad = DPAD // (2 * depth)
    tokens, cols = rhs.shape[1:]
    full = jax.ShapeDtypeStruct((depth, rows, cols), BF16)
    part = jax.ShapeDtypeStruct((depth // 2, rows, cols), BF16)
    order = [full, part, part, part, part, part, part]
    return pl.pallas_call(
        functools.partial(wgrad_plane_kernel, depth, rows, pad),
        out_shape=order,
        in_specs=[pl.BlockSpec(memory_space=pltpu.SMEM)] + vmem_specs(2),
        out_specs=vmem_specs(7),
        scratch_shapes=[pltpu.VMEM((2 * pad, cols), F32)],
        compiler_params=params(),
        cost_estimate=pl.CostEstimate(
            flops=4 * DPAD * tokens * cols, bytes_accessed=DPAD * (tokens + 4 * cols) * 2,
            transcendentals=0,
        ),
        name="wgrad_plane",
    )(ids, lhs, rhs)


def wgrad_all_kernel(depth, rows, pad, ids, lhs, rhs, own, oth, acc):
    dp_index, m = ids[0], ids[2]
    z, x = dp_index // 2, dp_index % 2

    def body(jz, carry):
        start = pl.multiple_of((z ^ jz) * (2 * pad), 2 * pad)
        left = lhs[pl.ds(start, 2 * pad), :]
        for jy in range(2):
            for jc in range(2):
                acc[...] = dot(left, rhs[m ^ (2 * jy + jc)])
                for jx in range(2):
                    block = acc[pl.ds(pl.multiple_of((x ^ jx) * pad, pad), rows), :]
                    (oth if jc else own)[jy, jx, jz] = block.astype(BF16)
        return carry

    lax.fori_loop(0, depth, body, 0)


def wgrad_all(lhs, rhs, ids, depth, rows):
    pad = DPAD // (2 * depth)
    tokens, cols = rhs.shape[1:]
    shape = jax.ShapeDtypeStruct((2, 2, depth, rows, cols), BF16)
    return pl.pallas_call(
        functools.partial(wgrad_all_kernel, depth, rows, pad),
        out_shape=[shape, shape],
        in_specs=[pl.BlockSpec(memory_space=pltpu.SMEM)] + vmem_specs(2),
        out_specs=vmem_specs(2),
        scratch_shapes=[pltpu.VMEM((2 * pad, cols), F32)],
        compiler_params=params(),
        cost_estimate=pl.CostEstimate(
            flops=8 * DPAD * tokens * cols, bytes_accessed=DPAD * (tokens + 8 * cols) * 2,
            transcendentals=0,
        ),
        name="wgrad_all",
    )(ids, lhs, rhs)


def scatter_all(links, own, oth):
    half = links.depth // 2
    got = links.over_core(oth)
    total = (own.astype(F32) + got.astype(F32)).astype(BF16)
    return links.scatter(
        (
            total[0, 0],
            total[0, 1, :half],
            total[0, 1, half:],
            total[1, 0, :half],
            total[1, 0, half:],
            total[1, 1, :half],
            total[1, 1, half:],
        )
    )


def transposed(value):
    return value.astype(F32).T.astype(BF16)


def mask_tile(segment_start, q_tile, k_tile, tokens):
    key = k_tile * TILE + lax.broadcasted_iota(jnp.int32, (TILE, TILE), 0)
    query = 2 * tokens + q_tile * TILE + lax.broadcasted_iota(jnp.int32, (TILE, TILE), 1)
    allowed = (key >= segment_start) & (key <= query)
    return jnp.where(allowed, 0.0, MASK_FILL)


def attend_kernel(tokens, first, seg, q, kv2, kv1, kv0, out, lse, q_t, k3, v_t, acc, peak, total, bias):
    q_t[...] = transposed(q[...])
    for s, kv in enumerate((kv2, kv1, kv0)):
        span = pl.ds(s * tokens, tokens)
        v_t[:, span] = transposed(kv[...])[KV_HEADS * HEAD_DIM :]
        for g in range(KV_HEADS):
            k3[g, span, :] = kv[:, g * HEAD_DIM : (g + 1) * HEAD_DIM]
    acc[...] = jnp.zeros_like(acc)
    peak[...] = jnp.full_like(peak, MASK_FILL)
    total[...] = jnp.zeros_like(total)
    for i in range(tokens // TILE):
        cols = pl.ds(i * TILE, TILE)

        def step(t, carry):
            bias[...] = mask_tile(seg[0:1, cols], i, t, tokens)
            keys = pl.ds(pl.multiple_of(t * TILE, TILE), TILE)

            def group(g, carry):
                k_g = k3[g, keys, :]
                v_g = v_t[pl.ds(pl.multiple_of(g * HEAD_DIM, HEAD_DIM), HEAD_DIM), keys]
                for j in range(GROUP):
                    h = g * GROUP + j
                    rows = pl.ds(pl.multiple_of(h * HEAD_DIM, HEAD_DIM), HEAD_DIM)
                    scores = dot(k_g, q_t[rows, cols]) + bias[...]
                    old = peak[pl.ds(h, 1), cols]
                    new = jnp.maximum(old, jnp.max(scores, axis=0, keepdims=True))
                    probs = jnp.exp2(scores * EXP_SCALE - new * EXP_SCALE)
                    scale = jnp.exp2((old - new) * EXP_SCALE)
                    peak[pl.ds(h, 1), cols] = new
                    total[pl.ds(h, 1), cols] = total[pl.ds(h, 1), cols] * scale + jnp.sum(
                        probs, axis=0, keepdims=True
                    )
                    acc[rows, cols] = acc[rows, cols] * scale + dot(v_g, probs.astype(BF16))
                return carry

            return lax.fori_loop(0, KV_HEADS, group, carry)

        lax.fori_loop(first[i], i + 2 * tokens // TILE + 1, step, 0)
    for h in range(HEADS):
        rows = pl.ds(h * HEAD_DIM, HEAD_DIM)
        acc[rows, :] = acc[rows, :] / total[h : h + 1, :]
    out[...] = acc[...].T.astype(BF16)
    lse[...] = peak[...] * EXP_SCALE + jnp.log2(jnp.maximum(total[...], 1e-37))


def attend(first, seg, q, kv2, kv1, kv0):
    tokens, width = q.shape
    window = 3 * tokens
    return pl.pallas_call(
        functools.partial(attend_kernel, tokens),
        out_shape=[
            jax.ShapeDtypeStruct((tokens, width), BF16),
            jax.ShapeDtypeStruct((HEADS + 1, tokens), F32),
        ],
        in_specs=[pl.BlockSpec(memory_space=pltpu.SMEM)] + vmem_specs(5),
        out_specs=vmem_specs(2),
        scratch_shapes=[
            pltpu.VMEM((width, tokens), BF16),
            pltpu.VMEM((KV_HEADS, window, HEAD_DIM), BF16),
            pltpu.VMEM((KV_HEADS * HEAD_DIM, window), BF16),
            pltpu.VMEM((width, tokens), F32),
            pltpu.VMEM((HEADS + 1, tokens), F32),
            pltpu.VMEM((HEADS + 1, tokens), F32),
            pltpu.VMEM((TILE, TILE), F32),
        ],
        compiler_params=params(),
        cost_estimate=pl.CostEstimate(
            flops=16 << 30, bytes_accessed=6 << 20, transcendentals=8 << 20
        ),
        name="attend",
    )(first, seg, q, kv2, kv1, kv0)


def attend_back_kernel(
    tokens, first, seg, q, kv2, kv1, kv0, grad, lse, delta,
    dq, d2, d1, d0,
    q_t, g_t, q3, g3, k3, v3, k_t, dq_t, dk, dv, bias,
):
    q_t[...] = transposed(q[...])
    g_t[...] = transposed(grad[...])
    for h in range(HEADS):
        q3[h] = q[:, h * HEAD_DIM : (h + 1) * HEAD_DIM]
        g3[h] = grad[:, h * HEAD_DIM : (h + 1) * HEAD_DIM]
    for s, kv in enumerate((kv2, kv1, kv0)):
        span = pl.ds(s * tokens, tokens)
        k_t[:, span] = transposed(kv[...])[: KV_HEADS * HEAD_DIM]
        for g in range(KV_HEADS):
            k3[g, span, :] = kv[:, g * HEAD_DIM : (g + 1) * HEAD_DIM]
            v3[g, span, :] = kv[:, (KV_HEADS + g) * HEAD_DIM : (KV_HEADS + g + 1) * HEAD_DIM]
    dq_t[...] = jnp.zeros_like(dq_t)
    dk[...] = jnp.zeros_like(dk)
    dv[...] = jnp.zeros_like(dv)
    for i in range(tokens // TILE):
        cols = pl.ds(i * TILE, TILE)

        def step(t, carry):
            bias[...] = mask_tile(seg[0:1, cols], i, t, tokens)
            keys = pl.ds(pl.multiple_of(t * TILE, TILE), TILE)

            def group(g, carry):
                k_g = k3[g, keys, :]
                v_g = v3[g, keys, :]
                kt_g = k_t[pl.ds(pl.multiple_of(g * HEAD_DIM, HEAD_DIM), HEAD_DIM), keys]
                for j in range(GROUP):
                    h = g * GROUP + j
                    rows = pl.ds(pl.multiple_of(h * HEAD_DIM, HEAD_DIM), HEAD_DIM)
                    scores = dot(k_g, q_t[rows, cols]) * EXP_SCALE + bias[...]
                    probs = jnp.exp2(scores - lse[pl.ds(h, 1), cols])
                    dprobs = dot(v_g, g_t[rows, cols])
                    dscores = (probs * (dprobs - delta[pl.ds(h, 1), cols])).astype(BF16)
                    dv[g, keys, :] += dot(probs.astype(BF16), g3[h, cols, :])
                    dk[g, keys, :] += dot(dscores, q3[h, cols, :])
                    dq_t[rows, cols] += dot(kt_g, dscores)
                return carry

            return lax.fori_loop(0, KV_HEADS, group, carry)

        lax.fori_loop(first[i], i + 2 * tokens // TILE + 1, step, 0)
    dq[...] = dq_t[...].T * SCORE_SCALE
    for s, out in enumerate((d2, d1, d0)):
        span = pl.ds(s * tokens, tokens)
        for g in range(KV_HEADS):
            out[:, g * HEAD_DIM : (g + 1) * HEAD_DIM] = (dk[g, span, :] * SCORE_SCALE).astype(
                out.dtype
            )
            out[:, (KV_HEADS + g) * HEAD_DIM : (KV_HEADS + g + 1) * HEAD_DIM] = dv[
                g, span, :
            ].astype(out.dtype)


def attend_back(first, seg, q, kv2, kv1, kv0, grad, lse, delta):
    tokens, width = q.shape
    window = 3 * tokens
    kv_width = kv0.shape[1]
    return pl.pallas_call(
        functools.partial(attend_back_kernel, tokens),
        out_shape=[
            jax.ShapeDtypeStruct((tokens, width), F32),
            jax.ShapeDtypeStruct((tokens, kv_width), BF16),
            jax.ShapeDtypeStruct((tokens, kv_width), BF16),
            jax.ShapeDtypeStruct((tokens, kv_width), F32),
        ],
        in_specs=[pl.BlockSpec(memory_space=pltpu.SMEM)] + vmem_specs(8),
        out_specs=vmem_specs(4),
        scratch_shapes=[
            pltpu.VMEM((width, tokens), BF16),
            pltpu.VMEM((width, tokens), BF16),
            pltpu.VMEM((HEADS, tokens, HEAD_DIM), BF16),
            pltpu.VMEM((HEADS, tokens, HEAD_DIM), BF16),
            pltpu.VMEM((KV_HEADS, window, HEAD_DIM), BF16),
            pltpu.VMEM((KV_HEADS, window, HEAD_DIM), BF16),
            pltpu.VMEM((KV_HEADS * HEAD_DIM, window), BF16),
            pltpu.VMEM((width, tokens), F32),
            pltpu.VMEM((KV_HEADS, window, HEAD_DIM), F32),
            pltpu.VMEM((KV_HEADS, window, HEAD_DIM), F32),
            pltpu.VMEM((TILE, TILE), F32),
        ],
        compiler_params=params(),
        cost_estimate=pl.CostEstimate(
            flops=32 << 30, bytes_accessed=10 << 20, transcendentals=8 << 20
        ),
        name="attend_back",
    )(first, seg, q, kv2, kv1, kv0, grad, lse, delta)


def mean_square(value, width):
    return jnp.sum(value * value, axis=-1, keepdims=True) / width


def norm_back(values_in, inverse, gain, upstream, width):
    scaled = upstream * gain
    mean = jnp.sum(scaled * values_in, axis=-1, keepdims=True) / width
    grad_in = inverse * (scaled - values_in * inverse * inverse * mean)
    return grad_in, jnp.sum(upstream * values_in * inverse, axis=0)


def rotary_tables(position_ids):
    half_dim = HEAD_DIM // 2
    frequency = jnp.exp(
        jnp.arange(half_dim, dtype=F32) * (-2.0 * math.log(10000.0) / HEAD_DIM)
    )
    angles = position_ids.astype(F32)[:, None] * frequency[None, :]
    return jnp.cos(angles)[:, None, :], jnp.sin(angles)[:, None, :]


def rotate(tensor, cosine, sine):
    first, second = jnp.split(tensor, 2, axis=-1)
    return jnp.concatenate(
        [first * cosine - second * sine, second * cosine + first * sine], axis=-1
    )


def per_device(
    hidden_in, cotangent, segments, positions, attn_in, attn_out, w_gate, w_up, w_down,
    norm1_gain, norm2_gain,
):
    tokens, width = hidden_in.shape[1:]
    dp_size = lax.axis_size("dp")
    links = Links(dp_size)
    depth = links.depth
    rows = width // dp_size
    pad = DPAD // dp_size
    dp_index, m = lax.axis_index("dp"), lax.axis_index("mp")
    core = m % 2
    ids = jnp.stack([dp_index, m // 2, m]).astype(jnp.int32)
    query_cols, kv_cols = HEADS * HEAD_DIM, KV_HEADS * HEAD_DIM

    def padded(value):
        value = value.reshape(value.shape[0], dp_size, rows)
        return jnp.pad(value, ((0, 0), (0, 0), (0, pad - rows))).reshape(-1, DPAD)

    def unpadded(value):
        return value.reshape(-1, dp_size, pad)[:, :, :rows].reshape(-1, width)

    in_blocks = links.gather(attn_in)
    gains_z = [jnp.stack([norm1_gain, norm2_gain])]
    gains_z += [links.over_z(gains_z[0], k) for k in range(1, depth)]
    gains_own = jnp.stack(gains_z)
    gains = jnp.stack([gains_own, links.over_x(gains_own)], axis=1).reshape(dp_size, 2, rows)
    gains = jnp.take(gains, dp_index ^ jnp.arange(dp_size), axis=0).transpose(1, 0, 2)
    gains = padded(gains.reshape(2, width)).astype(F32)
    gain_one, gain_two = gains[0], gains[1]
    out_blocks = links.gather(attn_out.T)
    gate_blocks = links.gather(w_gate)
    up_blocks = links.gather(w_up)
    down_blocks = links.gather(w_down.T)

    def all_columns(blocks):
        own = assemble(blocks, ids)
        other = links.over_core(own)
        first = jnp.where(core == 0, own, other)
        second = jnp.where(core == 0, other, own)
        return jnp.concatenate([first[0], second[0], first[1], second[1]], axis=1)

    resid_in = padded(hidden_in[0]).astype(F32)
    cot = padded(cotangent[0])
    cot_other = links.over_core(cot)
    inv_one = lax.rsqrt(mean_square(resid_in, width) + EPSILON)
    normed1_b = (resid_in * inv_one * gain_one).astype(BF16)
    qkv_weight = all_columns(in_blocks)
    projected = dot(normed1_b, qkv_weight)
    cosine, sine = rotary_tables(positions[0])
    turned = rotate(
        projected[:, : query_cols + kv_cols].reshape(tokens, HEADS + KV_HEADS, HEAD_DIM),
        cosine,
        sine,
    ).astype(BF16).reshape(tokens, query_cols + kv_cols)
    queries = turned[:, :query_cols]
    kv0 = jnp.concatenate(
        [turned[:, query_cols:], projected[:, query_cols + kv_cols :].astype(BF16)], axis=1
    )
    kv2 = links.some(kv0, {0: 2, 1: 3})
    kv1 = links.some(kv0, {0: 1, 2: 3})
    kv1 = jnp.where(m == 2, links.some(kv2, {3: 2}), kv1)

    seq_seg = segments[0]
    own_seg = lax.dynamic_slice_in_dim(seq_seg, m * tokens, tokens, 0)
    start = jnp.sum(seq_seg[None, :] < own_seg[:, None], axis=1, dtype=jnp.int32)
    start = start - (m - 2) * tokens
    first = start.reshape(-1, TILE)[:, 0] // TILE
    seg = start[None, :]
    attn_b, lse = attend(first, seg, queries, kv2, kv1, kv0)
    out_weight_t = all_columns(out_blocks)
    middle = resid_in + dot_nt(attn_b, out_weight_t)
    inv_two = lax.rsqrt(mean_square(middle, width) + EPSILON)
    normed2_b = (middle * inv_two * gain_two).astype(BF16)

    def columns(blocks):
        pair = assemble(blocks, ids)
        return jnp.concatenate([pair[0], pair[1]], axis=1)

    gate_w, up_w, down_t = columns(gate_blocks), columns(up_blocks), columns(down_blocks)
    both_normed = jnp.concatenate([normed2_b, links.over_core(normed2_b)], axis=0)
    both_cot = jnp.concatenate([cot, cot_other], axis=0)
    gate = dot(both_normed, gate_w)
    upper = dot(both_normed, up_w)
    sigma = jax.nn.sigmoid(gate)
    silu_gate = gate * sigma
    hidden_b = (silu_gate * upper).astype(BF16)
    ffn = dot_nt(hidden_b, down_t)
    ffn_own = ffn[:tokens] + links.over_core(ffn[tokens:].astype(BF16)).astype(F32)
    hidden_out = unpadded((middle + ffn_own).astype(BF16))

    def halves(value):
        return value.reshape(value.shape[0], 2, -1).transpose(1, 0, 2)

    down_parts = wgrad_plane(both_cot.T, halves(hidden_b), ids, depth, rows)
    grad_hid = dot(both_cot, down_t)
    grad_gate_act = (grad_hid * upper * sigma * (1.0 + gate * (1.0 - sigma))).astype(BF16)
    grad_up_act = (grad_hid * silu_gate).astype(BF16)
    grad_n2 = dot_nt(grad_gate_act, gate_w) + dot_nt(grad_up_act, up_w)
    grad_n2 = grad_n2[:tokens] + links.over_core(grad_n2[tokens:].astype(BF16)).astype(F32)
    normed2_t = both_normed.T
    gate_parts = wgrad_plane(normed2_t, halves(grad_gate_act), ids, depth, rows)
    up_parts = wgrad_plane(normed2_t, halves(grad_up_act), ids, depth, rows)
    g_down = links.scatter(down_parts)
    g_gate = links.scatter(gate_parts)
    g_up = links.scatter(up_parts)

    grad_mid_norm, g_gain2 = norm_back(middle, inv_two, gain_two, grad_n2, width)
    grad_middle = cot.astype(F32) + grad_mid_norm
    middle_b = grad_middle.astype(BF16)
    quarters = lambda value: value.reshape(value.shape[0], 4, -1).transpose(1, 0, 2)
    g_out_parts = wgrad_all(middle_b.T, quarters(attn_b), ids, depth, rows)
    g_out = scatter_all(links, *g_out_parts)
    grad_attn = dot(middle_b, out_weight_t).astype(BF16)
    delta = jnp.sum(
        (grad_attn.astype(F32) * attn_b.astype(F32)).reshape(tokens, HEADS, HEAD_DIM), axis=-1
    ).T
    delta = jnp.pad(delta, ((0, 1), (0, 0)))

    grad_q, part2, part1, part0 = attend_back(
        first, seg, queries, kv2, kv1, kv0, grad_attn, lse, delta
    )
    passed = links.some(part1, {2: 3})
    part2 = (part2.astype(F32) + passed.astype(F32)).astype(BF16)
    grad_kv = (
        part0
        + links.some(part1, {1: 0, 3: 2}).astype(F32)
        + links.some(part2, {2: 0, 3: 1}).astype(F32)
    )
    turned_back = rotate(
        jnp.concatenate([grad_q, grad_kv[:, :kv_cols]], axis=1).reshape(
            tokens, HEADS + KV_HEADS, HEAD_DIM
        ),
        cosine,
        -sine,
    ).reshape(tokens, query_cols + kv_cols)
    grad_proj = jnp.concatenate([turned_back, grad_kv[:, kv_cols:]], axis=1).astype(BF16)
    g_in_parts = wgrad_all(normed1_b.T, quarters(grad_proj), ids, depth, rows)
    g_in = scatter_all(links, *g_in_parts)
    grad_n1 = dot_nt(grad_proj, qkv_weight)
    grad_in_norm, g_gain1 = norm_back(resid_in, inv_one, gain_one, grad_n1, width)
    grad_input = unpadded(grad_middle + grad_in_norm)
    g_gains = links.all_sum(jnp.stack([g_gain1, g_gain2]))
    g_gains = lax.dynamic_slice_in_dim(g_gains, dp_index * pad, rows, 1)
    return (
        hidden_out[None],
        grad_input[None],
        g_in,
        g_out.T,
        g_gate,
        g_up,
        g_down.T,
        g_gains[0],
        g_gains[1],
    )


def solution(mesh):
    return jax.shard_map(
        per_device,
        mesh=mesh,
        in_specs=(
            P("dp", "mp", None),
            P("dp", "mp", None),
            P("dp", None),
            P("dp", "mp"),
            P("dp", "mp"),
            P("mp", "dp"),
            P("dp", "mp"),
            P("dp", "mp"),
            P("mp", "dp"),
            P("dp"),
            P("dp"),
        ),
        out_specs=(
            P("dp", "mp", None),
            P("dp", "mp", None),
            P("dp", "mp"),
            P("mp", "dp"),
            P("dp", "mp"),
            P("dp", "mp"),
            P("mp", "dp"),
            P("dp"),
            P("dp"),
        ),
        check_vma=False,
    )
```

time: 1200 us -> 629 us (0.52)
  waiting for transfers between devices: 722 us -> 121 us
  matrix products: 261 us -> 58.3 us
  starting transfers between devices: 1.66 us -> 189 us
  blocking collectives: 115 us -> 0 us
  Pallas kernels: 0 us -> 92.5 us
  local copies, waits for them, and re-layouts: 13.4 us -> 104 us
  other arithmetic: 65.6 us -> 50 us
  between operations: 16.4 us -> 2.26 us
    unnamed x26 -> x0, waiting for transfers between devices: 391 us -> none
    dot_general x49 -> x10, matrix products: 257 us -> 58.3 us  [the longest x5 29.5 us: dot(): return jnp.dot(a, b, preferred_element_type=F32)]
    reduce_scatter x5 -> x0, waiting for transfers between devices: 190 us -> none  [the longest x1 61.8 us: per_device(): lax.psum_scatter(jnp.dot(grad_gate_act, gate_weight.T, preferred_element_...]
    ppermute x0 -> x103, starting transfers between devices: none -> 189 us  [send(): return lax.ppermute(value, ('dp', 'mp'), self.pairs(move))]
    all_gather x9 -> x0, waiting for transfers between devices: 141 us -> none  [the longest x1 35.4 us: per_device(): lax.all_gather(w_gate, 'dp', axis=0, tiled=True)]
    ppermute x0 -> x103, waiting for transfers between devices: none -> 121 us  [send(): return lax.ppermute(value, ('dp', 'mp'), self.pairs(move))]
    pallas_call x0 -> x12, Pallas kernels: none -> 92.5 us  [the longest x3 24.1 us: wgrad_plane(): pl.pallas_call(functools.partial(wgrad_plane_kernel, depth, rows, pad), o...]
    all_gather x2 -> x0, blocking collectives: 67.5 us -> none  [the longest x1 34.3 us: per_device(): lax.all_gather(attn_in, 'dp', axis=0, tiled=True)]
  transfers between devices with their start and end apart: 20 -> 103, of which waited for: 16 -> 37; matrix products, arithmetic and copies ran while one was open for 17% -> 24% of each run, Pallas kernels for 0% -> 11%
where the time goes in v1:
time: 629 us; the launch traced here: 618 us
  starting transfers between devices  189 us (30%)
  waiting for transfers between devices  121 us (19%)
  local copies, waits for them, and re-layouts  104 us (17%)
  Pallas kernels  92.5 us (15%)
  matrix products  58.3 us (9%)
  other arithmetic  50 us (8%)
    ppermute x103, starting transfers between devices, send(): return lax.ppermute(value, ('dp', 'mp'), self.pairs(move))  189 us
    ppermute x103, waiting for transfers between devices, send(): return lax.ppermute(value, ('dp', 'mp'), self.pairs(move))  121 us
    dot_general x5, matrix products, dot(): return jnp.dot(a, b, preferred_element_type=F32)  29.5 us
    dot_general x5, matrix products, dot_nt(): lax.dot_general(a, b, (((1,), (1,)), ((), ())), preferred_element_type=F32)  28.8 us
    pallas_call x3, Pallas kernels, wgrad_plane(): pl.pallas_call(functools.partial(wgrad_plane_kernel, depth, rows, pad), o...  24.1 us
    pallas_call x1, Pallas kernels, attend_back(): pl.pallas_call(functools.partial(attend_back_kernel, tokens), out_shape=[...  21.8 us
    pallas_call x1, Pallas kernels, attend(): pl.pallas_call(functools.partial(attend_kernel, tokens), out_shape=[jax.S...  18.3 us
    pallas_call x5, Pallas kernels, assemble(): pl.pallas_call(functools.partial(assemble_kernel, depth, rows, pad), out_...  16.1 us
  transfers between devices with their start and end apart: 103, of which 37 were waited for; matrix products, arithmetic and copies ran while one was open for 24% of the time, Pallas kernels for 11%

profile of v1, /device:TPU:0, one launch (start us, length us, event | category | flops | bytes accessed | tf_op | source)
XLA Modules:
  0.0 617.6 jit_solution(17829009041901547406)
XLA Ops:
  21.3 6.6 %collective-permute-done.8.by_y = bf16[4,120,400]{2,1,0:T(8,128)(2,1)S(1)} collective-permute-done((bf16[4,120,400]{2,1,0:T(8,128)(2,1)S(1)}, bf16[4,120,400]{2,1,0:T(8,128)(2,1)S(1)}, u32[]{:S(2)}, u32[]{:S(2)}) %collective-permute-start.8) | collective-permute-done | bytes 384032 | tf_op jit(solution)/shard_map/ppermute | solution.py:57
  63.3 6.0 collective-permute-done.32
  73.1 5.6 collective-permute-start.40
  82.0 4.5 collective-permute-start.24
  91.3 7.4 %collective-permute-done.25 = bf16[120,640]{1,0:T(8,128)(2,1)S(1)} collective-permute-done((bf16[120,640]{1,0:T(8,128)(2,1)S(1)}, bf16[120,640]{1,0:T(8,128)(2,1)S(1)}, u32[]{:S(2)}, u32[]{:S(2)}) %collective-permute-start.25) | collective-permute-done | bytes 153632 | tf_op jit(solution)/shard_map/ppermute | solution.py:57
  122.6 6.8 %concatenate.52 = bf16[1024,1600]{1,0:T(8,128)(2,1)} concatenate(bf16[1024,400]{1,0:T(8,128)(2,1)} %get-tuple-element.206, bf16[1024,400]{1,0:T(8,128)(2,1)S(1)} %get-tuple-element.160, bf16[1024,400]{1,0:T(8,128)(2,1)} %get-tuple-element.207, bf16[1024,400]{1,0:T(8,128)(2,1)S(1)} %get-tuple-element.159), dimensions={1} | concatenate | bytes 6553600 | tf_op jit(solution)/shard_map/concatenate | solution.py:486
  164.9 8.5 %collective-permute-done.43.low = bf16[2,120,640]{2,1,0:T(8,128)(2,1)S(1)} collective-permute-done((bf16[2,120,640]{2,1,0:T(8,128)(2,1)S(1)}, bf16[2,120,640]{2,1,0:T(8,128)(2,1)S(1)}, u32[]{:S(2)}, u32[]{:S(2)}) %collective-permute-start.43) | collective-permute-done | bytes 307232 | tf_op jit(solution)/shard_map/ppermute | solution.py:57
  197.9 18.3 %attend.1 = (bf16[512,960]{1,0:T(8,128)(2,1)}, f32[16,512]{1,0:T(8,128)}) custom-call(s32[2]{0:T(128)} %and_select_fusion.first, s32[1,512]{1,0:T(1,128)} %bitcast.341, bf16[512,960]{1,0:T(8,128)(2,1)} %copy.200.q, bf16[512,640]{1,0:T(8,128)(2,1)} %collective-permute-done.12.kv2, bf16[512,640]{1,0:T(8,128)(2,1)} %broadcast_select_fusion.4.kv1, ...), custom_call_target="tpu_custom_call" | custom-call | flops 17179869184 | bytes 6291456 | tf_op jit(solution)/shard_map/attend/pallas_call | solution.py:302
  220.0 10.7 %collective-permute-start.23 = (bf16[512,1024]{0,1:T(8,128)(2,1)}, bf16[512,1024]{0,1:T(8,128)(2,1)}, u32[]{:S(2)}, u32[]{:S(2)}) collective-permute-start(bf16[512,1024]{0,1:T(8,128)(2,1)} %multiply_convert_fusion.3), channel_id=1, source_target_pairs={{0,1},{1,0},{2,3},{3,2},{4,5},{5,4},{6,7},{7,6},{8,9},{9,8},{10,11... | collective-permute-start | bytes 3145736 | tf_op jit(solution)/shard_map/ppermute | solution.py:57
  233.2 6.5 %fusion.14 = f32[1024,1280]{1,0:T(8,128)} fusion(bf16[1024,640]{1,0:T(8,128)(2,1)S(1)} %get-tuple-element.151, bf16[1024,640]{1,0:T(8,128)(2,1)S(1)} %get-tuple-element.150, bf16[512,1024]{0,1:T(8,128)(2,1)} %collective-permute-done.46, bf16[512,1024]{0,1:T(8,128)(2,1)S(1)} %bitcast.284), kind=kOutput, calls=%fused_computation.49 | convolution fusion | flops 2693791744 | bytes 9961472 | tf_op jit(solution)/shard_map/dot_general | solution.py:27
  244.4 5.5 fusion.17
  249.9 10.1 %multiply_convert_fusion.1 = (bf16[1024,1280]{1,0:T(8,128)(2,1)}, bf16[1024,1280]{1,0:T(8,128)(2,1)}, bf16[1024,1280]{1,0:T(8,128)(2,1)S(1)}) fusion(f32[1024,1280]{1,0:T(8,128)} %fusion.14, f32[1024,1280]{1,0:T(8,128)S(1)} %fusion.17, bf16[1024,640]{1,0:T(8,128)(2,1)S(1)} %copy-done.21, bf16[1024,640]{1,0:T(8,128)(2,1)S(1)} %copy-done.20, ...), kind=kOutput, calls=%fused_computation.2 | convolution fusion | flops 2713452544 | bytes 23068672 | tf_op jit(solution)/shard_map/dot_general | solution.py:27
  261.5 4.4 fusion.15
  266.0 4.5 copy.192
  270.4 7.5 %fusion.16 = f32[1024,1024]{0,1:T(8,128)} fusion(bf16[1024,1280]{1,0:T(8,128)(2,1)} %get-tuple-element.142, bf16[1024,640]{1,0:T(8,128)(2,1)} %get-tuple-element.155, bf16[1024,640]{1,0:T(8,128)(2,1)} %get-tuple-element.154), kind=kOutput, calls=%fused_computation.51 | convolution fusion | flops 2689597440 | bytes 9437184 | tf_op jit(solution)/shard_map/dot_general | solution.py:31
  277.9 4.5 copy.190
  291.2 7.9 %wgrad_plane.5 = (bf16[4,120,640]{2,1,0:T(8,128)(2,1)}, bf16[2,120,640]{2,1,0:T(8,128)(2,1)}, bf16[2,120,640]{2,1,0:T(8,128)(2,1)}, bf16[2,120,640]{2,1,0:T(8,12...) custom-call(s32[3]{0:T(128)} %pad_add_fusion.ids, ...), custom_call_target="tpu_custom_call" | custom-call | flops 2684354560 | bytes 7340032 | tf_op jit(solution)/shard_map/wgrad_plane/pallas_call | solution.py:174
  301.2 8.2 %collective-permute-start.93 = (bf16[2,120,640]{2,1,0:T(8,128)(2,1)}, bf16[2,120,640]{2,1,0:T(8,128)(2,1)S(1)}, u32[]{:S(2)}, u32[]{:S(2)}) collective-permute-start(bf16[2,120,640]{2,1,0:T(8,128)(2,1)} %get-tuple-element.70), channel_id=1, source_target_pairs={{0,4},{1,5},{2,6},{3,7},{4,0},{5,1},{6,2},{7,3},{8,12},{9,13},{10,... | collective-permute-start | bytes 921608 | tf_op jit(solution)/shard_map/ppermute | solution.py:57
  313.8 8.7 %convolution_add_fusion = f32[1024,1024]{0,1:T(8,128)} fusion(f32[1024,1024]{0,1:T(8,128)} %fusion.16, bf16[1024,1280]{1,0:T(8,128)(2,1)} %get-tuple-element.141, bf16[1024,640]{1,0:T(8,128)(2,1)} %get-tuple-element.153, bf16[1024,640]{1,0:T(8,128)(2,1)} %get-tuple-element.152), kind=kOutput, calls=%fused_computation.48 | convolution fusion | flops 2690646016 | bytes 13631488 | tf_op jit(solution)/shard_map/dot_general | solution.py:31
  325.6 7.8 %wgrad_plane.4 = (bf16[4,120,640]{2,1,0:T(8,128)(2,1)}, bf16[2,120,640]{2,1,0:T(8,128)(2,1)}, bf16[2,120,640]{2,1,0:T(8,128)(2,1)}, bf16[2,120,640]{2,1,0:T(8,12...) custom-call(s32[3]{0:T(128)} %pad_add_fusion.ids, ...), custom_call_target="tpu_custom_call" | custom-call | flops 2684354560 | bytes 7340032 | tf_op jit(solution)/shard_map/wgrad_plane/pallas_call | solution.py:174
  333.5 4.5 copy.188
  342.4 8.4 %wgrad_plane.3 = (bf16[4,120,640]{2,1,0:T(8,128)(2,1)}, bf16[2,120,640]{2,1,0:T(8,128)(2,1)}, bf16[2,120,640]{2,1,0:T(8,128)(2,1)}, bf16[2,120,640]{2,1,0:T(8,12...) custom-call(s32[3]{0:T(128)} %pad_add_fusion.ids, ...), custom_call_target="tpu_custom_call" | custom-call | flops 2684354560 | bytes 7340032 | tf_op jit(solution)/shard_map/wgrad_plane/pallas_call | solution.py:174
  392.7 4.7 collective-permute-done.85
  405.4 11.7 %collective-permute-start.95 = (bf16[120,640]{1,0:T(8,128)(2,1)S(1)}, bf16[120,640]{1,0:T(8,128)(2,1)S(1)}, u32[]{:S(2)}, u32[]{:S(2)}) collective-permute-start(bf16[120,640]{1,0:T(8,128)(2,1)S(1)} %get-tuple-element.179), channel_id=1, source_target_pairs={{0,8},{1,9},{2,10},{3,11},{4,12},{5,13},{6,14},{7,15},{8,0},{9,1},... | collective-permute-start | bytes 460808 | tf_op jit(solution)/shard_map/ppermute | solution.py:57
  424.0 10.8 %collective-permute-done.96 = bf16[120,640]{1,0:T(8,128)(2,1)S(1)} collective-permute-done((bf16[120,640]{1,0:T(8,128)(2,1)S(1)}, bf16[120,640]{1,0:T(8,128)(2,1)S(1)}, u32[]{:S(2)}, u32[]{:S(2)}) %collective-permute-start.96) | collective-permute-done | bytes 153632 | tf_op jit(solution)/shard_map/ppermute | solution.py:57
  450.1 5.0 wgrad_all.3
  455.1 21.8 %attend_back.1 = (f32[512,960]{1,0:T(8,128)}, bf16[512,640]{1,0:T(8,128)(2,1)}, bf16[512,640]{1,0:T(8,128)(2,1)}, f32[512,640]{1,0:T(8,128)}) custom-call(s32[2]{0:T(128)} %and_select_fusion.first, s32[1,512]{1,0:T(1,128)} %bitcast.342, bf16[512,960]{1,0:T(8,128)(2,1)} %copy.200.q, bf16[512,640]{1,0:T(8,128)(2,1)} %collective-permute-done.12.kv2, ...), custom_call_target="tpu_custom_call" | custom-call | flops 34359738368 | bytes 10485760 | tf_op jit(solution)/shard_map/attend_back/pallas_call | solution.py:388
  483.5 27.2 %collective-permute-start.63 = (bf16[2,120,240]{2,1,0:T(8,128)(2,1)S(1)}, bf16[2,120,240]{2,1,0:T(8,128)(2,1)S(1)}, u32[]{:S(2)}, u32[]{:S(2)}) collective-permute-start(bf16[2,120,240]{2,1,0:T(8,128)(2,1)S(1)} %get-tuple-element.176), channel_id=1, source_target_pairs={{0,2},{1,3},{2,0},{3,1},{4,6},{5,7},{6,4},{7,5},{8,10},{9,11},{10,... | collective-permute-start | bytes 345608 | tf_op jit(solution)/shard_map/ppermute | solution.py:57
  524.6 12.6 %collective-permute-done.62 = bf16[2,120,240]{2,1,0:T(8,128)(2,1)S(1)} collective-permute-done((bf16[2,120,240]{2,1,0:T(8,128)(2,1)S(1)}, bf16[2,120,240]{2,1,0:T(8,128)(2,1)S(1)}, u32[]{:S(2)}, u32[]{:S(2)}) %collective-permute-start.62) | collective-permute-done | bytes 115232 | tf_op jit(solution)/shard_map/ppermute | solution.py:57
  551.9 7.2 %wgrad_all.2 = (bf16[2,2,4,120,400]{4,3,2,1,0:T(8,128)(2,1)}, bf16[2,2,4,120,400]{4,3,2,1,0:T(8,128)(2,1)}) custom-call(s32[3]{0:T(128)} %pad_add_fusion.ids, bf16[1024,512]{1,0:T(8,128)(2,1)} %bitcast.299, bf16[4,512,400]{2,1,0:T(8,128)(2,1)} %bitcast.297), custom_call_target="tpu_custom_call" | custom-call | flops 1677721600 | bytes 7602176 | tf_op jit(solution)/shard_map/wgrad_all/pallas_call | solution.py:211
  563.3 5.6 fusion.13
  590.2 5.5 collective-permute-done.53
  (522 shorter events, 340.3 us)
Async XLA Ops:
  8.6 40.2 %collective-permute-start.2 = (bf16[2,120]{1,0:T(2,128)(2,1)}, bf16[2,120]{1,0:T(2,128)(2,1)S(1)}, u32[]{:S(2)}, u32[]{:S(2)}) collective-permute-start(bf16[2,120]{1,0:T(2,128)(2,1)} %pad_maximum_fusion.29), channel_id=1, source_target_pairs={{0,24},{1,25},{2,26},{3,27},{4,28},{5,29},{6,30},{7,31},{8,16},{9,... | collective-permute-start | bytes 1448 | tf_op jit(solution)/shard_map/ppermute | solution.py:57
  12.4 37.3 %collective-permute-start = (bf16[2,120]{1,0:T(2,128)(2,1)}, bf16[2,120]{1,0:T(2,128)(2,1)S(1)}, u32[]{:S(2)}, u32[]{:S(2)}) collective-permute-start(bf16[2,120]{1,0:T(2,128)(2,1)} %pad_maximum_fusion.29), channel_id=1, source_target_pairs={{0,8},{1,9},{2,10},{3,11},{4,12},{5,13},{6,14},{7,15},{8,0},{9,1},... | collective-permute-start | bytes 1448 | tf_op jit(solution)/shard_map/ppermute | solution.py:57
  15.3 34.5 %collective-permute-start.1 = (bf16[2,120]{1,0:T(2,128)(2,1)}, bf16[2,120]{1,0:T(2,128)(2,1)S(1)}, u32[]{:S(2)}, u32[]{:S(2)}) collective-permute-start(bf16[2,120]{1,0:T(2,128)(2,1)} %pad_maximum_fusion.29), channel_id=1, source_target_pairs={{0,16},{1,17},{2,18},{3,19},{4,20},{5,21},{6,22},{7,23},{8,24},{9,... | collective-permute-start | bytes 1448 | tf_op jit(solution)/shard_map/ppermute | solution.py:57
  49.8 64.1 %collective-permute-start.11 = (bf16[2,1024,400]{1,2,0:T(8,128)(2,1)}, bf16[2,1024,400]{1,2,0:T(8,128)(2,1)}, u32[]{:S(2)}, u32[]{:S(2)}) collective-permute-start(bf16[2,1024,400]{1,2,0:T(8,128)(2,1)} %copy.167), channel_id=1, source_target_pairs={{0,1},{1,0},{2,3},{3,2},{4,5},{5,4},{6,7},{7,6},{8,9},{9,8},{10,11... | collective-permute-start | bytes 4915208 | tf_op jit(solution)/shard_map/ppermute | solution.py:57
  79.3 31.8 %collective-permute-start.34 = (bf16[4,120,640]{2,1,0:T(8,128)(2,1)}, bf16[4,120,640]{2,1,0:T(8,128)(2,1)}, u32[]{:S(2)}, u32[]{:S(2)}) collective-permute-start(bf16[4,120,640]{2,1,0:T(8,128)(2,1)} %pad_maximum_fusion.18.own), channel_id=1, source_target_pairs={{0,4},{1,5},{2,6},{3,7},{4,0},{5,1},{6,2},{7,3},{8,12},{9,13},{10,... | collective-permute-start | bytes 1843208 | tf_op jit(solution)/shard_map/ppermute | solution.py:57
  91.2 57.7 %collective-permute-start.46 = (bf16[512,1024]{0,1:T(8,128)(2,1)S(1)}, bf16[512,1024]{0,1:T(8,128)(2,1)}, u32[]{:S(2)}, u32[]{:S(2)}) collective-permute-start(bf16[512,1024]{0,1:T(8,128)(2,1)S(1)} %bitcast.282), channel_id=1, source_target_pairs={{0,1},{1,0},{2,3},{3,2},{4,5},{5,4},{6,7},{7,6},{8,9},{9,8},{10,11... | collective-permute-start | bytes 3145736 | tf_op jit(solution)/shard_map/ppermute | solution.py:57
  104.8 29.0 %collective-permute-start.35 = (bf16[4,120,640]{2,1,0:T(8,128)(2,1)}, bf16[4,120,640]{2,1,0:T(8,128)(2,1)}, u32[]{:S(2)}, u32[]{:S(2)}) collective-permute-start(bf16[4,120,640]{2,1,0:T(8,128)(2,1)} %pad_maximum_fusion.18.own), channel_id=1, source_target_pairs={{0,2},{1,3},{2,0},{3,1},{4,6},{5,7},{6,4},{7,5},{8,10},{9,11},{10,... | collective-permute-start | bytes 1843208 | tf_op jit(solution)/shard_map/ppermute | solution.py:57
  105.7 32.9 %collective-permute-start.41 = (bf16[4,120,640]{2,1,0:T(8,128)(2,1)}, bf16[4,120,640]{2,1,0:T(8,128)(2,1)}, u32[]{:S(2)}, u32[]{:S(2)}) collective-permute-start(bf16[4,120,640]{2,1,0:T(8,128)(2,1)} %pad_maximum_fusion.19.own), channel_id=1, source_target_pairs={{0,4},{1,5},{2,6},{3,7},{4,0},{5,1},{6,2},{7,3},{8,12},{9,13},{10,... | collective-permute-start | bytes 1843208 | tf_op jit(solution)/shard_map/ppermute | solution.py:57
  111.1 27.5 %collective-permute-start.42 = (bf16[4,120,640]{2,1,0:T(8,128)(2,1)}, bf16[4,120,640]{2,1,0:T(8,128)(2,1)}, u32[]{:S(2)}, u32[]{:S(2)}) collective-permute-start(bf16[4,120,640]{2,1,0:T(8,128)(2,1)} %pad_maximum_fusion.19.own), channel_id=1, source_target_pairs={{0,2},{1,3},{2,0},{3,1},{4,6},{5,7},{6,4},{7,5},{8,10},{9,11},{10,... | collective-permute-start | bytes 1843208 | tf_op jit(solution)/shard_map/ppermute | solution.py:57
  113.9 26.0 %collective-permute-start.27 = (bf16[4,120,640]{2,1,0:T(8,128)(2,1)}, bf16[4,120,640]{2,1,0:T(8,128)(2,1)}, u32[]{:S(2)}, u32[]{:S(2)}) collective-permute-start(bf16[4,120,640]{2,1,0:T(8,128)(2,1)} %pad_maximum_fusion.17.own), channel_id=1, source_target_pairs={{0,4},{1,5},{2,6},{3,7},{4,0},{5,1},{6,2},{7,3},{8,12},{9,13},{10,... | collective-permute-start | bytes 1843208 | tf_op jit(solution)/shard_map/ppermute | solution.py:57
  138.6 52.0 %collective-permute-start.22 = (bf16[2,1024,240]{1,2,0:T(8,128)(2,1)}, bf16[2,1024,240]{1,2,0:T(8,128)(2,1)}, u32[]{:S(2)}, u32[]{:S(2)}) collective-permute-start(bf16[2,1024,240]{1,2,0:T(8,128)(2,1)} %copy.174), channel_id=1, source_target_pairs={{0,1},{1,0},{2,3},{3,2},{4,5},{5,4},{6,7},{7,6},{8,9},{9,8},{10,11... | collective-permute-start | bytes 2949128 | tf_op jit(solution)/shard_map/ppermute | solution.py:57
  139.9 37.2 %collective-permute-start.12 = (bf16[512,640]{1,0:T(8,128)(2,1)}, bf16[512,640]{1,0:T(8,128)(2,1)}, u32[]{:S(2)}, u32[]{:S(2)}) collective-permute-start(bf16[512,640]{1,0:T(8,128)(2,1)} %pad_maximum_fusion.16.kv0), channel_id=1, source_target_pairs={{0,2},{1,3},{4,6},{5,7},{8,10},{9,11},{12,14},{13,15},{16,18},{17,... | collective-permute-start | bytes 1966088 | tf_op jit(solution)/shard_map/ppermute | solution.py:57
  148.9 24.4 %collective-permute-start.43 = (bf16[2,120,640]{2,1,0:T(8,128)(2,1)S(1)}, bf16[2,120,640]{2,1,0:T(8,128)(2,1)S(1)}, u32[]{:S(2)}, u32[]{:S(2)}) collective-permute-start(bf16[2,120,640]{2,1,0:T(8,128)(2,1)S(1)} %slice.349), channel_id=1, source_target_pairs={{0,2},{1,3},{2,0},{3,1},{4,6},{5,7},{6,4},{7,5},{8,10},{9,11},{10,... | collective-permute-start | bytes 921608 | tf_op jit(solution)/shard_map/ppermute | solution.py:57
  158.9 26.8 %collective-permute-start.29 = (bf16[2,120,640]{2,1,0:T(8,128)(2,1)S(1)}, bf16[2,120,640]{2,1,0:T(8,128)(2,1)S(1)}, u32[]{:S(2)}, u32[]{:S(2)}) collective-permute-start(bf16[2,120,640]{2,1,0:T(8,128)(2,1)S(1)} %slice.341), channel_id=1, source_target_pairs={{0,2},{1,3},{2,0},{3,1},{4,6},{5,7},{6,4},{7,5},{8,10},{9,11},{10,... | collective-permute-start | bytes 921608 | tf_op jit(solution)/shard_map/ppermute | solution.py:57
  285.1 155.1 %collective-permute-start.45 = (bf16[512,1024]{0,1:T(8,128)(2,1)}, bf16[512,1024]{0,1:T(8,128)(2,1)}, u32[]{:S(2)}, u32[]{:S(2)}) collective-permute-start(bf16[512,1024]{0,1:T(8,128)(2,1)} %slice.508), channel_id=1, source_target_pairs={{0,1},{1,0},{2,3},{3,2},{4,5},{5,4},{6,7},{7,6},{8,9},{9,8},{10,11... | collective-permute-start | bytes 3145736 | tf_op jit(solution)/shard_map/ppermute | solution.py:57
  299.1 51.9 %collective-permute-start.90 = (bf16[2,120,640]{2,1,0:T(8,128)(2,1)}, bf16[2,120,640]{2,1,0:T(8,128)(2,1)}, u32[]{:S(2)}, u32[]{:S(2)}) collective-permute-start(bf16[2,120,640]{2,1,0:T(8,128)(2,1)} %get-tuple-element.67), channel_id=1, source_target_pairs={{0,2},{1,3},{2,0},{3,1},{4,6},{5,7},{6,4},{7,5},{8,10},{9,11},{10,... | collective-permute-start | bytes 921608 | tf_op jit(solution)/shard_map/ppermute | solution.py:57
  299.1 74.1 %collective-permute-start.89 = (bf16[2,120,640]{2,1,0:T(8,128)(2,1)}, bf16[2,120,640]{2,1,0:T(8,128)(2,1)}, u32[]{:S(2)}, u32[]{:S(2)}) collective-permute-start(bf16[2,120,640]{2,1,0:T(8,128)(2,1)} %get-tuple-element.65), channel_id=1, source_target_pairs={{0,2},{1,3},{2,0},{3,1},{4,6},{5,7},{6,4},{7,5},{8,10},{9,11},{10,... | collective-permute-start | bytes 921608 | tf_op jit(solution)/shard_map/ppermute | solution.py:57
  301.2 53.0 %collective-permute-start.93 = (bf16[2,120,640]{2,1,0:T(8,128)(2,1)}, bf16[2,120,640]{2,1,0:T(8,128)(2,1)S(1)}, u32[]{:S(2)}, u32[]{:S(2)}) collective-permute-start(bf16[2,120,640]{2,1,0:T(8,128)(2,1)} %get-tuple-element.70), channel_id=1, source_target_pairs={{0,4},{1,5},{2,6},{3,7},{4,0},{5,1},{6,2},{7,3},{8,12},{9,13},{10,... | collective-permute-start | bytes 921608 | tf_op jit(solution)/shard_map/ppermute | solution.py:57
  309.3 70.4 %collective-permute-start.92 = (bf16[2,120,640]{2,1,0:T(8,128)(2,1)}, bf16[2,120,640]{2,1,0:T(8,128)(2,1)}, u32[]{:S(2)}, u32[]{:S(2)}) collective-permute-start(bf16[2,120,640]{2,1,0:T(8,128)(2,1)} %get-tuple-element.68), channel_id=1, source_target_pairs={{0,4},{1,5},{2,6},{3,7},{4,0},{5,1},{6,2},{7,3},{8,12},{9,13},{10,... | collective-permute-start | bytes 921608 | tf_op jit(solution)/shard_map/ppermute | solution.py:57
  379.7 55.9 %collective-permute-start.47 = (bf16[512,1024]{0,1:T(8,128)(2,1)S(1)}, bf16[512,1024]{0,1:T(8,128)(2,1)S(1)}, u32[]{:S(2)}, u32[]{:S(2)}) collective-permute-start(bf16[512,1024]{0,1:T(8,128)(2,1)S(1)} %slice.507), channel_id=1, source_target_pairs={{0,1},{1,0},{2,3},{3,2},{4,5},{5,4},{6,7},{7,6},{8,9},{9,8},{10,11... | collective-permute-start | bytes 3145736 | tf_op jit(solution)/shard_map/ppermute | solution.py:57
  391.3 26.6 %collective-permute-start.74 = (bf16[2,120,640]{2,1,0:T(8,128)(2,1)S(1)}, bf16[2,120,640]{2,1,0:T(8,128)(2,1)S(1)}, u32[]{:S(2)}, u32[]{:S(2)}) collective-permute-start(bf16[2,120,640]{2,1,0:T(8,128)(2,1)S(1)} %copy-done.80), channel_id=1, source_target_pairs={{0,4},{1,5},{2,6},{3,7},{4,0},{5,1},{6,2},{7,3},{8,12},{9,13},{10,... | collective-permute-start | bytes 921608 | tf_op jit(solution)/shard_map/ppermute | solution.py:57
  422.4 54.5 %collective-permute-start.86 = (bf16[120,640]{1,0:T(8,128)(2,1)}, bf16[120,640]{1,0:T(8,128)(2,1)}, u32[]{:S(2)}, u32[]{:S(2)}) collective-permute-start(bf16[120,640]{1,0:T(8,128)(2,1)} %get-tuple-element.182), channel_id=1, source_target_pairs={{0,8},{1,9},{2,10},{3,11},{4,12},{5,13},{6,14},{7,15},{8,0},{9,1},... | collective-permute-start | bytes 460808 | tf_op jit(solution)/shard_map/ppermute | solution.py:57
  434.8 44.8 %collective-permute-start.87 = (bf16[120,640]{1,0:T(8,128)(2,1)}, bf16[120,640]{1,0:T(8,128)(2,1)}, u32[]{:S(2)}, u32[]{:S(2)}) collective-permute-start(bf16[120,640]{1,0:T(8,128)(2,1)} %get-tuple-element.184), channel_id=1, source_target_pairs={{0,16},{1,17},{2,18},{3,19},{4,20},{5,21},{6,22},{7,23},{8,24},{9,... | collective-permute-start | bytes 460808 | tf_op jit(solution)/shard_map/ppermute | solution.py:57
  434.8 45.7 %collective-permute-start.88 = (bf16[120,640]{1,0:T(8,128)(2,1)}, bf16[120,640]{1,0:T(8,128)(2,1)}, u32[]{:S(2)}, u32[]{:S(2)}) collective-permute-start(bf16[120,640]{1,0:T(8,128)(2,1)} %get-tuple-element.183), channel_id=1, source_target_pairs={{0,24},{1,25},{2,26},{3,27},{4,28},{5,29},{6,30},{7,31},{8,16},{9,... | collective-permute-start | bytes 460808 | tf_op jit(solution)/shard_map/ppermute | solution.py:57
  435.6 81.4 %collective-permute-start.77 = (bf16[120,640]{1,0:T(8,128)(2,1)}, bf16[120,640]{1,0:T(8,128)(2,1)}, u32[]{:S(2)}, u32[]{:S(2)}) collective-permute-start(bf16[120,640]{1,0:T(8,128)(2,1)} %get-tuple-element.185), channel_id=1, source_target_pairs={{0,8},{1,9},{2,10},{3,11},{4,12},{5,13},{6,14},{7,15},{8,0},{9,1},... | collective-permute-start | bytes 460808 | tf_op jit(solution)/shard_map/ppermute | solution.py:57
  455.1 28.1 %collective-permute-start.61 = (bf16[2,2,4,120,240]{4,3,2,1,0:T(8,128)(2,1)}, bf16[2,2,4,120,240]{4,3,2,1,0:T(8,128)(2,1)S(1)}, u32[]{:S(2)}, u32[]{:S(2)}) collective-permute-start(bf16[2,2,4,120,240]{4,3,2,1,0:T(8,128)(2,1)} %get-tuple-element.49), channel_id=1, source_target_pairs={{0,1},{1,0},{2,3},{3,2},{4,5},{5,4},{6,7},{7,6},{8,9},{9,8},{10,11... | collective-permute-start | bytes 2764808 | tf_op jit(solution)/shard_map/ppermute | solution.py:57
  476.9 42.8 %collective-permute-start.78 = (bf16[120,640]{1,0:T(8,128)(2,1)S(1)}, bf16[120,640]{1,0:T(8,128)(2,1)S(1)}, u32[]{:S(2)}, u32[]{:S(2)}) collective-permute-start(bf16[120,640]{1,0:T(8,128)(2,1)S(1)} %get-tuple-element.187), channel_id=1, source_target_pairs={{0,16},{1,17},{2,18},{3,19},{4,20},{5,21},{6,22},{7,23},{8,24},{9,... | collective-permute-start | bytes 460808 | tf_op jit(solution)/shard_map/ppermute | solution.py:57
  479.6 40.1 %collective-permute-start.79 = (bf16[120,640]{1,0:T(8,128)(2,1)S(1)}, bf16[120,640]{1,0:T(8,128)(2,1)S(1)}, u32[]{:S(2)}, u32[]{:S(2)}) collective-permute-start(bf16[120,640]{1,0:T(8,128)(2,1)S(1)} %get-tuple-element.186), channel_id=1, source_target_pairs={{0,24},{1,25},{2,26},{3,27},{4,28},{5,29},{6,30},{7,31},{8,16},{9,... | collective-permute-start | bytes 460808 | tf_op jit(solution)/shard_map/ppermute | solution.py:57
  480.5 30.2 %collective-permute-start.49 = (bf16[512,640]{1,0:T(8,128)(2,1)}, bf16[512,640]{1,0:T(8,128)(2,1)S(1)}, u32[]{:S(2)}, u32[]{:S(2)}) collective-permute-start(bf16[512,640]{1,0:T(8,128)(2,1)} %get-tuple-element.44), channel_id=1, source_target_pairs={{2,3},{6,7},{10,11},{14,15},{18,19},{22,23},{26,27},{30,31}} | collective-permute-start | bytes 1966088 | tf_op jit(solution)/shard_map/ppermute | solution.py:57
  483.5 30.1 %collective-permute-start.63 = (bf16[2,120,240]{2,1,0:T(8,128)(2,1)S(1)}, bf16[2,120,240]{2,1,0:T(8,128)(2,1)S(1)}, u32[]{:S(2)}, u32[]{:S(2)}) collective-permute-start(bf16[2,120,240]{2,1,0:T(8,128)(2,1)S(1)} %get-tuple-element.176), channel_id=1, source_target_pairs={{0,2},{1,3},{2,0},{3,1},{4,6},{5,7},{6,4},{7,5},{8,10},{9,11},{10,... | collective-permute-start | bytes 345608 | tf_op jit(solution)/shard_map/ppermute | solution.py:57
  513.6 29.2 %collective-permute-start.48 = (bf16[512,640]{1,0:T(8,128)(2,1)S(1)}, bf16[512,640]{1,0:T(8,128)(2,1)S(1)}, u32[]{:S(2)}, u32[]{:S(2)}) collective-permute-start(bf16[512,640]{1,0:T(8,128)(2,1)S(1)} %copy-done.79), channel_id=1, source_target_pairs={{1,0},{3,2},{5,4},{7,6},{9,8},{11,10},{13,12},{15,14},{17,16},{19,... | collective-permute-start | bytes 1966088 | tf_op jit(solution)/shard_map/ppermute | solution.py:57
  515.6 27.2 %collective-permute-start.50 = (bf16[512,640]{1,0:T(8,128)(2,1)S(1)}, bf16[512,640]{1,0:T(8,128)(2,1)S(1)}, u32[]{:S(2)}, u32[]{:S(2)}) collective-permute-start(bf16[512,640]{1,0:T(8,128)(2,1)S(1)} %add_convert_fusion.2), channel_id=1, source_target_pairs={{2,0},{3,1},{6,4},{7,5},{10,8},{11,9},{14,12},{15,13},{18,16},{19,... | collective-permute-start | bytes 1966088 | tf_op jit(solution)/shard_map/ppermute | solution.py:57
  (158 other events, 1972.2 us)

commit v2 on v1

--- a/solution.py
+++ b/solution.py
@@ -70,15 +70,6 @@
 
     def some(self, value, table):
         return self.send(value, lambda d, m: (d, table[m]) if m in table else None)
-
-    def gather(self, value):
-        half = self.depth // 2
-        own = jnp.stack([value] + [self.over_z(value, k) for k in range(1, self.depth)])
-        by_x = self.over_x(own)
-        by_y = self.over_y(own)
-        low = self.over_y(by_x[:half])
-        high = self.over_x(by_y[half:])
-        return own, by_x, by_y, low, high
 
     def scatter(self, parts):
         p00, p01a, p01b, p10a, p10b, p11a, p11b = parts
@@ -110,37 +101,6 @@
         return value
 
 
-def assemble_kernel(depth, rows, pad, ids, own, by_x, by_y, low, high, out):
-    dp_index, y = ids[0], ids[1]
-    half = depth // 2
-    out[...] = jnp.zeros_like(out)
-    for jz in range(depth):
-        for jx in range(2):
-            for jy in range(2):
-                if jx and jy:
-                    block = low[jz] if jz < half else high[jz - half]
-                else:
-                    block = (by_x if jx else by_y if jy else own)[jz]
-                start = pl.multiple_of((dp_index ^ (2 * jz + jx)) * pad, pad)
-                out[y ^ jy, pl.ds(start, rows), :] = block
-
-
-def assemble(blocks, ids):
-    depth, rows, cols = blocks[0].shape
-    pad = DPAD // (2 * depth)
-    return pl.pallas_call(
-        functools.partial(assemble_kernel, depth, rows, pad),
-        out_shape=jax.ShapeDtypeStruct((2, DPAD, cols), BF16),
-        in_specs=[pl.BlockSpec(memory_space=pltpu.SMEM)] + vmem_specs(5),
-        out_specs=pl.BlockSpec(memory_space=pltpu.VMEM),
-        compiler_params=params(),
-        cost_estimate=pl.CostEstimate(
-            flops=0, bytes_accessed=DPAD * cols * 8, transcendentals=0
-        ),
-        name="assemble",
-    )(ids, *blocks)
-
-
 def wgrad_plane_kernel(depth, rows, pad, ids, lhs, rhs, *refs):
     outs, acc = refs[:-1], refs[-1]
     dp_index, y = ids[0], ids[1]
@@ -150,12 +110,12 @@
 
         def body(i, carry):
             jz = part * half + i
-            start = pl.multiple_of((z ^ jz) * (2 * pad), 2 * pad)
-            left = lhs[pl.ds(start, 2 * pad), :]
-            for jy in range(2):
-                acc[...] = dot(left, rhs[y ^ jy])
-                for jx in range(2):
-                    block = acc[pl.ds(pl.multiple_of((x ^ jx) * pad, pad), rows), :]
+            for jx in range(2):
+                start = pl.multiple_of(((x ^ jx) * depth + (z ^ jz)) * pad, pad)
+                left = lhs[pl.ds(start, pad), :]
+                for jy in range(2):
+                    acc[...] = dot(left, rhs[y ^ jy])
+                    block = acc[pl.ds(0, rows), :]
                     if jy == 0 and jx == 0:
                         outs[0][jz] = block.astype(BF16)
                     else:
@@ -176,7 +136,7 @@
         out_shape=order,
         in_specs=[pl.BlockSpec(memory_space=pltpu.SMEM)] + vmem_specs(2),
         out_specs=vmem_specs(7),
-        scratch_shapes=[pltpu.VMEM((2 * pad, cols), F32)],
+        scratch_shapes=[pltpu.VMEM((pad, cols), F32)],
         compiler_params=params(),
         cost_estimate=pl.CostEstimate(
             flops=4 * DPAD * tokens * cols, bytes_accessed=DPAD * (tokens + 4 * cols) * 2,
@@ -191,13 +151,13 @@
     z, x = dp_index // 2, dp_index % 2
 
     def body(jz, carry):
-        start = pl.multiple_of((z ^ jz) * (2 * pad), 2 * pad)
-        left = lhs[pl.ds(start, 2 * pad), :]
-        for jy in range(2):
-            for jc in range(2):
-                acc[...] = dot(left, rhs[m ^ (2 * jy + jc)])
-                for jx in range(2):
-                    block = acc[pl.ds(pl.multiple_of((x ^ jx) * pad, pad), rows), :]
+        for jx in range(2):
+            start = pl.multiple_of(((x ^ jx) * depth + (z ^ jz)) * pad, pad)
+            left = lhs[pl.ds(start, pad), :]
+            for jy in range(2):
+                for jc in range(2):
+                    acc[...] = dot(left, rhs[m ^ (2 * jy + jc)])
+                    block = acc[pl.ds(0, rows), :]
                     (oth if jc else own)[jy, jx, jz] = block.astype(BF16)
         return carry
 
@@ -213,7 +173,7 @@
         out_shape=[shape, shape],
         in_specs=[pl.BlockSpec(memory_space=pltpu.SMEM)] + vmem_specs(2),
         out_specs=vmem_specs(2),
-        scratch_shapes=[pltpu.VMEM((2 * pad, cols), F32)],
+        scratch_shapes=[pltpu.VMEM((pad, cols), F32)],
         compiler_params=params(),
         cost_estimate=pl.CostEstimate(
             flops=8 * DPAD * tokens * cols, bytes_accessed=DPAD * (tokens + 8 * cols) * 2,
@@ -244,84 +204,315 @@
     return value.astype(F32).T.astype(BF16)
 
 
-def mask_tile(segment_start, q_tile, k_tile, tokens):
-    key = k_tile * TILE + lax.broadcasted_iota(jnp.int32, (TILE, TILE), 0)
-    query = 2 * tokens + q_tile * TILE + lax.broadcasted_iota(jnp.int32, (TILE, TILE), 1)
-    allowed = (key >= segment_start) & (key <= query)
-    return jnp.where(allowed, 0.0, MASK_FILL)
-
-
-def attend_kernel(tokens, first, seg, q, kv2, kv1, kv0, out, lse, q_t, k3, v_t, acc, peak, total, bias):
-    q_t[...] = transposed(q[...])
-    for s, kv in enumerate((kv2, kv1, kv0)):
-        span = pl.ds(s * tokens, tokens)
-        v_t[:, span] = transposed(kv[...])[KV_HEADS * HEAD_DIM :]
-        for g in range(KV_HEADS):
-            k3[g, span, :] = kv[:, g * HEAD_DIM : (g + 1) * HEAD_DIM]
+class Place:
+    def __init__(self, depth, send_sems, recv_sems):
+        dp_index, m = lax.axis_index("dp"), lax.axis_index("mp")
+        self.depth = depth
+        self.z, self.x = dp_index // 2, dp_index % 2
+        self.m, self.y, self.c = m, m // 2, m % 2
+        self.send_sems, self.recv_sems = send_sems, recv_sems
+        self.count = 0
+
+    def peer(self, kind):
+        z, x, y, c = self.z, self.x, self.y, self.c
+        if kind == "x":
+            x = 1 - x
+        elif kind == "y":
+            y = 1 - y
+        elif kind == "c":
+            c = 1 - c
+        else:
+            z = (z + kind) % self.depth
+        return 2 * z + x, 2 * y + c
+
+    def kinds(self):
+        return ["x", "y", "c"] + list(range(1, self.depth))
+
+    def barrier(self):
+        semaphore = pltpu.get_barrier_semaphore()
+        for kind in self.kinds():
+            pl.semaphore_signal(
+                semaphore, inc=1, device_id=self.peer(kind), device_id_type=pl.DeviceIdType.MESH
+            )
+        pl.semaphore_wait(semaphore, len(self.kinds()))
+
+    def copy(self, kind, source, target=None):
+        index = self.count
+        self.count += 1
+        made = pltpu.make_async_remote_copy(
+            src_ref=source,
+            dst_ref=source if target is None else target,
+            send_sem=self.send_sems.at[index],
+            recv_sem=self.recv_sems.at[index],
+            device_id=self.peer(kind),
+            device_id_type=pl.DeviceIdType.MESH,
+        )
+        made.start()
+        return made
+
+
+class PlaneGather:
+    def __init__(self, place, source, buffer, diagonal_by_x=False):
+        self.place, self.source, self.buffer = place, source, buffer
+        self.diagonal_by_x = diagonal_by_x
+        self.sent = []
+
+    def over_z(self):
+        p = self.place
+        slot = self.buffer.at[p.y, p.x, p.z]
+        self.arriving = [p.copy(k, self.source, slot) for k in range(1, p.depth)]
+        self.sent += self.arriving
+
+    def over_xy(self):
+        p = self.place
+        for made in self.arriving:
+            made.wait_recv()
+        own = self.buffer.at[p.y, p.x]
+        self.by_x, self.by_y = p.copy("x", own), p.copy("y", own)
+        self.sent += [self.by_x, self.by_y]
+
+    def diagonal(self):
+        p = self.place
+        half = p.depth // 2
+        self.by_x.wait_recv()
+        if self.diagonal_by_x:
+            self.by_y.wait_recv()
+            self.last = [p.copy("x", self.buffer.at[1 - p.y, p.x])]
+        else:
+            low = p.copy("y", self.buffer.at[p.y, 1 - p.x, pl.ds(0, half)])
+            self.by_y.wait_recv()
+            self.last = [low, p.copy("x", self.buffer.at[1 - p.y, p.x, pl.ds(half, half)])]
+        self.sent += self.last
+
+    def arrived(self):
+        for made in self.last:
+            made.wait_recv()
+
+    def finish(self):
+        for made in self.sent:
+            made.wait_send()
+
+
+def rope(value, cosine, sine):
+    lane = lax.broadcasted_iota(jnp.int32, value.shape, 1)
+    half = HEAD_DIM // 2
+    partner = jnp.where(
+        lane % HEAD_DIM < half, pltpu.roll(value, 128 - half, 1), pltpu.roll(value, half, 1)
+    )
+    return value * cosine + partner * sine
+
+
+def mean_rows(value, width):
+    return jnp.sum(value, axis=-1, keepdims=True) * (1.0 / width)
+
+
+def mask_tile(start, query_tile, key_tile):
+    key = key_tile * TILE + lax.broadcasted_iota(jnp.int32, (TILE, TILE), 0)
+    query = query_tile * TILE + lax.broadcasted_iota(jnp.int32, (TILE, TILE), 1)
+    return jnp.where((key >= start) & (key <= query), 0.0, MASK_FILL)
+
+
+def front_kernel(
+    depth, rows, width, in_cols,
+    pack_a, pack_g, x_in, cosine, sine, seg,
+    q, kv, attn, lse, middle, normed1, normed2, gains, attn_w, ffn_w,
+    a_buf, proj, q_t, k3, v_t, acc, peak, total, bias, send_sems, recv_sems, local_sems,
+):
+    tokens = x_in.shape[0]
+    tiles = tokens // TILE
+    back = 1024 // TILE
+    pad = DPAD // (2 * depth)
+    p = Place(depth, send_sems, recv_sems)
+    a_buf[p.c, p.y, p.x, p.z] = pack_a[...]
+    own = [
+        pltpu.make_async_copy(pack_g.at[w], ffn_w.at[w, p.y, p.x, p.z], local_sems.at[w])
+        for w in range(3)
+    ]
+    for made in own:
+        made.start()
+    p.barrier()
+    plane = PlaneGather(p, pack_a, a_buf.at[p.c])
+    gate, up, down = [
+        PlaneGather(p, pack_g.at[w], ffn_w.at[w], w == 2) for w in range(3)
+    ]
+    plane.over_z()
+    plane.over_xy()
+    gate.over_z()
+    plane.diagonal()
+    plane.arrived()
+    cross = p.copy("c", a_buf.at[p.c])
+    for made in own:
+        made.wait()
+    up.over_z()
+    gate.over_xy()
+    x_f = x_in[...].astype(F32)
+    inv_one = lax.rsqrt(mean_rows(x_f * x_f, width) + EPSILON)
+    cross.wait()
+    for b in range(2 * depth):
+        gains[:, b * pad : (b + 1) * pad] = a_buf[
+            0, 0, b // depth, b % depth, pl.ds(rows, 2), 0:pad
+        ].astype(F32)
+    normed1[...] = (x_f * inv_one * gains[0:1, :]).astype(BF16)
+
+    def project(r, carry):
+        span = pl.ds(pl.multiple_of(r * TILE, TILE), TILE)
+        for b in range(4):
+            weight = a_buf[b % 2, b // 2].reshape(DPAD, -1)[:, :in_cols]
+            proj[span, b * in_cols : (b + 1) * in_cols] = dot(normed1[span, :], weight)
+        for j in range((HEADS + KV_HEADS) * HEAD_DIM // 128):
+            lanes = slice(128 * j, 128 * (j + 1))
+            proj[span, lanes] = rope(proj[span, lanes], cosine[span, :], sine[span, :])
+        return carry
+
+    lax.fori_loop(0, tiles, project, 0)
+    query_cols = HEADS * HEAD_DIM
+    q[...] = proj[:, :query_cols].astype(BF16)
+    kv[p.m] = proj[:, query_cols : query_cols + 2 * KV_HEADS * HEAD_DIM].astype(BF16)
+    mine = kv.at[p.m]
+    kv_y, kv_c = p.copy("y", mine), p.copy("c", mine)
+    down.over_z()
+    q_t[...] = proj[:, :query_cols].T.astype(BF16)
     acc[...] = jnp.zeros_like(acc)
     peak[...] = jnp.full_like(peak, MASK_FILL)
     total[...] = jnp.zeros_like(total)
-    for i in range(tokens // TILE):
+
+    def spread(block):
+        span = pl.ds(pl.multiple_of(block * tokens, tokens), tokens)
+        k3_parts = kv[block]
+        v_t[:, span] = transposed(k3_parts)[KV_HEADS * HEAD_DIM :]
+        for g in range(KV_HEADS):
+            k3[g, span, :] = k3_parts[:, g * HEAD_DIM : (g + 1) * HEAD_DIM]
+
+    def attend_tile(i, t):
         cols = pl.ds(i * TILE, TILE)
-
+        bias[...] = mask_tile(seg[0:1, cols], p.m * tiles + i, t)
+        keys = pl.ds(pl.multiple_of(t * TILE, TILE), TILE)
+
+        def group(g, carry):
+            k_g = k3[g, keys, :]
+            v_g = v_t[pl.ds(pl.multiple_of(g * HEAD_DIM, HEAD_DIM), HEAD_DIM), keys]
+            heads = [g * GROUP + j for j in range(GROUP)]
+            places = [pl.ds(pl.multiple_of(h * HEAD_DIM, HEAD_DIM), HEAD_DIM) for h in heads]
+            old = [peak[pl.ds(h, 1), cols] for h in heads]
+            sums = [total[pl.ds(h, 1), cols] for h in heads]
+            accs = [acc[s, cols] for s in places]
+            scores = [dot(k_g, q_t[s, cols]) + bias[...] for s in places]
+            new = [jnp.maximum(o, jnp.max(s, axis=0, keepdims=True)) for o, s in zip(old, scores)]
+            probs = [jnp.exp2(s * EXP_SCALE - n * EXP_SCALE) for s, n in zip(scores, new)]
+            scale = [jnp.exp2((o - n) * EXP_SCALE) for o, n in zip(old, new)]
+            outs = [dot(v_g, b.astype(BF16)) for b in probs]
+            for j, h in enumerate(heads):
+                peak[pl.ds(h, 1), cols] = new[j]
+                total[pl.ds(h, 1), cols] = sums[j] * scale[j] + jnp.sum(
+                    probs[j], axis=0, keepdims=True
+                )
+                acc[places[j], cols] = accs[j] * scale[j] + outs[j]
+            return carry
+
+        lax.fori_loop(0, KV_HEADS, group, 0)
+
+    def attend_span(i, low, high):
         def step(t, carry):
-            bias[...] = mask_tile(seg[0:1, cols], i, t, tokens)
-            keys = pl.ds(pl.multiple_of(t * TILE, TILE), TILE)
-
-            def group(g, carry):
-                k_g = k3[g, keys, :]
-                v_g = v_t[pl.ds(pl.multiple_of(g * HEAD_DIM, HEAD_DIM), HEAD_DIM), keys]
-                for j in range(GROUP):
-                    h = g * GROUP + j
-                    rows = pl.ds(pl.multiple_of(h * HEAD_DIM, HEAD_DIM), HEAD_DIM)
-                    scores = dot(k_g, q_t[rows, cols]) + bias[...]
-                    old = peak[pl.ds(h, 1), cols]
-                    new = jnp.maximum(old, jnp.max(scores, axis=0, keepdims=True))
-                    probs = jnp.exp2(scores * EXP_SCALE - new * EXP_SCALE)
-                    scale = jnp.exp2((old - new) * EXP_SCALE)
-                    peak[pl.ds(h, 1), cols] = new
-                    total[pl.ds(h, 1), cols] = total[pl.ds(h, 1), cols] * scale + jnp.sum(
-                        probs, axis=0, keepdims=True
-                    )
-                    acc[rows, cols] = acc[rows, cols] * scale + dot(v_g, probs.astype(BF16))
-                return carry
-
-            return lax.fori_loop(0, KV_HEADS, group, carry)
-
-        lax.fori_loop(first[i], i + 2 * tokens // TILE + 1, step, 0)
+            attend_tile(i, t)
+            return carry
+
+        lax.fori_loop(low, high, step, 0)
+
+    spread(p.m)
+    first_tile = p.m * tiles
+    for i in range(tiles):
+        attend_span(i, first_tile, first_tile + i + 1)
+    kv_y.wait_recv()
+    kv_cy = p.copy("c", kv.at[(p.m + 2) % 4])
+    up.over_xy()
+    gate.diagonal()
+    kv_c.wait_recv()
+    kv_cy.wait_recv()
+    for k in range(1, 4):
+        spread((p.m + k) % 4)
+    for i in range(tiles):
+        attend_span(i, jnp.maximum(first_tile + i - back, 0), first_tile)
+        if i == 0:
+            down.over_xy()
+            up.diagonal()
     for h in range(HEADS):
-        rows = pl.ds(h * HEAD_DIM, HEAD_DIM)
-        acc[rows, :] = acc[rows, :] / total[h : h + 1, :]
-    out[...] = acc[...].T.astype(BF16)
+        span = pl.ds(h * HEAD_DIM, HEAD_DIM)
+        acc[span, :] = acc[span, :] / total[h : h + 1, :]
+    attn[...] = acc[...].T.astype(BF16)
     lse[...] = peak[...] * EXP_SCALE + jnp.log2(jnp.maximum(total[...], 1e-37))
-
-
-def attend(first, seg, q, kv2, kv1, kv0):
-    tokens, width = q.shape
-    window = 3 * tokens
+    saved = pltpu.make_async_copy(a_buf, attn_w, local_sems.at[0])
+    saved.start()
+    down.diagonal()
+    out_cols = query_cols // 4
+
+    def project_out(r, carry):
+        span = pl.ds(pl.multiple_of(r * TILE, TILE), TILE)
+        mid = x_in[span, :].astype(F32)
+        for b in range(4):
+            weight = a_buf[b % 2, b // 2].reshape(DPAD, -1)[:, in_cols : in_cols + out_cols]
+            mid += dot_nt(attn[span, b * out_cols : (b + 1) * out_cols], weight)
+        middle[span, :] = mid
+        inv = lax.rsqrt(mean_rows(mid * mid, width) + EPSILON)
+        normed2[span, :] = (mid * inv * gains[1:2, :]).astype(BF16)
+        return carry
+
+    lax.fori_loop(0, tiles, project_out, 0)
+    gate.arrived()
+    up.arrived()
+    down.arrived()
+    for part in (plane, gate, up, down):
+        part.finish()
+    for made in (kv_y, kv_c, kv_cy):
+        made.wait_send()
+    saved.wait()
+
+
+def front(pack_a, pack_g, x_in, cosine, sine, seg, depth, rows, width, in_cols):
+    tokens = x_in.shape[0]
+    pad = DPAD // (2 * depth)
+    cols = pack_a.shape[1]
+    query_cols, kv_cols = HEADS * HEAD_DIM, 2 * KV_HEADS * HEAD_DIM
+    whole = 4 * tokens
+    copies = 4 * (depth - 1) + 4 * 4 + 4
+    anywhere = pl.BlockSpec(memory_space=pl.ANY)
     return pl.pallas_call(
-        functools.partial(attend_kernel, tokens),
+        functools.partial(front_kernel, depth, rows, width, in_cols),
         out_shape=[
-            jax.ShapeDtypeStruct((tokens, width), BF16),
+            jax.ShapeDtypeStruct((tokens, query_cols), BF16),
+            jax.ShapeDtypeStruct((4, tokens, kv_cols), BF16),
+            jax.ShapeDtypeStruct((tokens, query_cols), BF16),
             jax.ShapeDtypeStruct((HEADS + 1, tokens), F32),
+            jax.ShapeDtypeStruct((tokens, DPAD), F32),
+            jax.ShapeDtypeStruct((tokens, DPAD), BF16),
+            jax.ShapeDtypeStruct((tokens, DPAD), BF16),
+            jax.ShapeDtypeStruct((2, DPAD), F32),
+            jax.ShapeDtypeStruct((2, 2, 2, depth, pad, cols), BF16),
+            jax.ShapeDtypeStruct((3, 2, 2, depth, pad, cols), BF16),
         ],
-        in_specs=[pl.BlockSpec(memory_space=pltpu.SMEM)] + vmem_specs(5),
-        out_specs=vmem_specs(2),
+        in_specs=vmem_specs(1) + [anywhere] + vmem_specs(4),
+        out_specs=vmem_specs(8) + [anywhere] * 2,
         scratch_shapes=[
-            pltpu.VMEM((width, tokens), BF16),
-            pltpu.VMEM((KV_HEADS, window, HEAD_DIM), BF16),
-            pltpu.VMEM((KV_HEADS * HEAD_DIM, window), BF16),
-            pltpu.VMEM((width, tokens), F32),
+            pltpu.VMEM((2, 2, 2, depth, pad, cols), BF16),
+            pltpu.VMEM((tokens, query_cols + kv_cols), F32),
+            pltpu.VMEM((query_cols, tokens), BF16),
+            pltpu.VMEM((KV_HEADS, whole, HEAD_DIM), BF16),
+            pltpu.VMEM((KV_HEADS * HEAD_DIM, whole), BF16),
+            pltpu.VMEM((query_cols, tokens), F32),
             pltpu.VMEM((HEADS + 1, tokens), F32),
             pltpu.VMEM((HEADS + 1, tokens), F32),
             pltpu.VMEM((TILE, TILE), F32),
+            pltpu.SemaphoreType.DMA((copies,)),
+            pltpu.SemaphoreType.DMA((copies,)),
+            pltpu.SemaphoreType.DMA((3,)),
         ],
-        compiler_params=params(),
+        compiler_params=pltpu.CompilerParams(
+            vmem_limit_bytes=58 << 20, collective_id=0, has_side_effects=True
+        ),
         cost_estimate=pl.CostEstimate(
-            flops=16 << 30, bytes_accessed=6 << 20, transcendentals=8 << 20
+            flops=20 << 30, bytes_accessed=40 << 20, transcendentals=8 << 20
         ),
-        name="attend",
-    )(first, seg, q, kv2, kv1, kv0)
+        name="front",
+    )(pack_a, pack_g, x_in, cosine, sine, seg)
 
 
 def attend_back_kernel(
@@ -347,7 +538,7 @@
         cols = pl.ds(i * TILE, TILE)
 
         def step(t, carry):
-            bias[...] = mask_tile(seg[0:1, cols], i, t, tokens)
+            bias[...] = mask_tile(seg[0:1, cols], i + 2 * tokens // TILE, t)
             keys = pl.ds(pl.multiple_of(t * TILE, TILE), TILE)
 
             def group(g, carry):
@@ -459,70 +650,53 @@
     query_cols, kv_cols = HEADS * HEAD_DIM, KV_HEADS * HEAD_DIM
 
     def padded(value):
-        value = value.reshape(value.shape[0], dp_size, rows)
-        return jnp.pad(value, ((0, 0), (0, 0), (0, pad - rows))).reshape(-1, DPAD)
+        value = value.reshape(value.shape[0], depth, 2, rows).transpose(0, 2, 1, 3)
+        return jnp.pad(value, ((0, 0), (0, 0), (0, 0), (0, pad - rows))).reshape(-1, DPAD)
 
     def unpadded(value):
-        return value.reshape(-1, dp_size, pad)[:, :, :rows].reshape(-1, width)
-
-    in_blocks = links.gather(attn_in)
-    gains_z = [jnp.stack([norm1_gain, norm2_gain])]
-    gains_z += [links.over_z(gains_z[0], k) for k in range(1, depth)]
-    gains_own = jnp.stack(gains_z)
-    gains = jnp.stack([gains_own, links.over_x(gains_own)], axis=1).reshape(dp_size, 2, rows)
-    gains = jnp.take(gains, dp_index ^ jnp.arange(dp_size), axis=0).transpose(1, 0, 2)
-    gains = padded(gains.reshape(2, width)).astype(F32)
-    gain_one, gain_two = gains[0], gains[1]
-    out_blocks = links.gather(attn_out.T)
-    gate_blocks = links.gather(w_gate)
-    up_blocks = links.gather(w_up)
-    down_blocks = links.gather(w_down.T)
-
-    def all_columns(blocks):
-        own = assemble(blocks, ids)
-        other = links.over_core(own)
-        first = jnp.where(core == 0, own, other)
-        second = jnp.where(core == 0, other, own)
-        return jnp.concatenate([first[0], second[0], first[1], second[1]], axis=1)
-
-    resid_in = padded(hidden_in[0]).astype(F32)
+        value = value.reshape(-1, 2, depth, pad)[..., :rows]
+        return value.transpose(0, 2, 1, 3).reshape(-1, width)
+
+    in_cols = attn_in.shape[1]
+    out_cols = attn_out.shape[0]
+    gains_in = jnp.pad(
+        jnp.stack([norm1_gain, norm2_gain]), ((0, pad - rows - 2), (0, in_cols + out_cols - rows))
+    )
+    pack_a = jnp.concatenate(
+        [jnp.concatenate([attn_in, attn_out.T], axis=1), gains_in], axis=0
+    )
+    pack_g = jnp.pad(jnp.stack([w_gate, w_up, w_down.T]), ((0, 0), (0, pad - rows), (0, 0)))
+    x_in = padded(hidden_in[0])
     cot = padded(cotangent[0])
-    cot_other = links.over_core(cot)
-    inv_one = lax.rsqrt(mean_square(resid_in, width) + EPSILON)
-    normed1_b = (resid_in * inv_one * gain_one).astype(BF16)
-    qkv_weight = all_columns(in_blocks)
-    projected = dot(normed1_b, qkv_weight)
     cosine, sine = rotary_tables(positions[0])
-    turned = rotate(
-        projected[:, : query_cols + kv_cols].reshape(tokens, HEADS + KV_HEADS, HEAD_DIM),
-        cosine,
-        sine,
-    ).astype(BF16).reshape(tokens, query_cols + kv_cols)
-    queries = turned[:, :query_cols]
-    kv0 = jnp.concatenate(
-        [turned[:, query_cols:], projected[:, query_cols + kv_cols :].astype(BF16)], axis=1
-    )
-    kv2 = links.some(kv0, {0: 2, 1: 3})
-    kv1 = links.some(kv0, {0: 1, 2: 3})
-    kv1 = jnp.where(m == 2, links.some(kv2, {3: 2}), kv1)
-
+    cos_lanes = jnp.tile(cosine[:, 0], (1, 4))
+    sin_lanes = jnp.tile(jnp.concatenate([-sine[:, 0], sine[:, 0]], axis=1), (1, 2))
     seq_seg = segments[0]
     own_seg = lax.dynamic_slice_in_dim(seq_seg, m * tokens, tokens, 0)
     start = jnp.sum(seq_seg[None, :] < own_seg[:, None], axis=1, dtype=jnp.int32)
+    queries, kv_all, attn_b, lse, middle, normed1_b, normed2_b, gains, attn_w, ffn_w = front(
+        pack_a, pack_g, x_in, cos_lanes, sin_lanes, start[None, :], depth, rows, width, in_cols
+    )
+    gain_one, gain_two = gains[0], gains[1]
+    attn_w = attn_w.reshape(2, 2, DPAD, -1)
+    attn_w = jnp.concatenate(
+        [attn_w[0, 0], attn_w[1, 0], attn_w[0, 1], attn_w[1, 1]], axis=1
+    ).reshape(DPAD, 4, -1)
+    qkv_weight = attn_w[:, :, :in_cols].reshape(DPAD, -1)
+    out_weight_t = attn_w[:, :, in_cols:].reshape(DPAD, -1)
+    resid_in = x_in.astype(F32)
+    inv_one = lax.rsqrt(mean_square(resid_in, width) + EPSILON)
+    inv_two = lax.rsqrt(mean_square(middle, width) + EPSILON)
+    cot_other = links.over_core(cot)
+    kv0 = lax.dynamic_index_in_dim(kv_all, m, 0, keepdims=False)
+    kv1 = lax.dynamic_index_in_dim(kv_all, jnp.maximum(m - 1, 0), 0, keepdims=False)
+    kv2 = lax.dynamic_index_in_dim(kv_all, jnp.maximum(m - 2, 0), 0, keepdims=False)
     start = start - (m - 2) * tokens
     first = start.reshape(-1, TILE)[:, 0] // TILE
     seg = start[None, :]
-    attn_b, lse = attend(first, seg, queries, kv2, kv1, kv0)
-    out_weight_t = all_columns(out_blocks)
-    middle = resid_in + dot_nt(attn_b, out_weight_t)
-    inv_two = lax.rsqrt(mean_square(middle, width) + EPSILON)
-    normed2_b = (middle * inv_two * gain_two).astype(BF16)
-
-    def columns(blocks):
-        pair = assemble(blocks, ids)
-        return jnp.concatenate([pair[0], pair[1]], axis=1)
-
-    gate_w, up_w, down_t = columns(gate_blocks), columns(up_blocks), columns(down_blocks)
+
+    ffn_w = ffn_w.reshape(3, 2, DPAD, -1)
+    gate_w, up_w, down_t = [jnp.concatenate([w[0], w[1]], axis=1) for w in ffn_w]
     both_normed = jnp.concatenate([normed2_b, links.over_core(normed2_b)], axis=0)
     both_cot = jnp.concatenate([cot, cot_other], axis=0)
     gate = dot(both_normed, gate_w)
@@ -586,7 +760,8 @@
     grad_in_norm, g_gain1 = norm_back(resid_in, inv_one, gain_one, grad_n1, width)
     grad_input = unpadded(grad_middle + grad_in_norm)
     g_gains = links.all_sum(jnp.stack([g_gain1, g_gain2]))
-    g_gains = lax.dynamic_slice_in_dim(g_gains, dp_index * pad, rows, 1)
+    position = (dp_index % 2) * depth + dp_index // 2
+    g_gains = lax.dynamic_slice_in_dim(g_gains, position * pad, rows, 1)
     return (
         hidden_out[None],
         grad_input[None],

time: 629 us -> 576 us (0.916)
  Pallas kernels: 92.5 us -> 187 us
  starting transfers between devices: 189 us -> 95.9 us
  waiting for transfers between devices: 121 us -> 98.7 us
  matrix products: 58.3 us -> 44.5 us
  local copies, waits for them, and re-layouts: 104 us -> 94.4 us
    pallas_call x6 -> x1, Pallas kernels: 34.4 us -> 130 us  [front(): pl.pallas_call(functools.partial(front_kernel, depth, rows, width, in_col...]
    ppermute x103 -> x59, starting transfers between devices: 189 us -> 95.9 us  [send(): return lax.ppermute(value, ('dp', 'mp'), self.pairs(move))]
    ppermute x103 -> x59, waiting for transfers between devices: 121 us -> 98.7 us  [send(): return lax.ppermute(value, ('dp', 'mp'), self.pairs(move))]
    dot_general x5 -> x4, matrix products: 29.5 us -> 20.7 us  [dot(): return jnp.dot(a, b, preferred_element_type=F32)]
    another operation x16 -> x7, other arithmetic: 10.9 us -> 2.46 us  [the longest x5 4.7 us: gather(): jnp.stack([value] + [self.over_z(value, k) for k in range(1, self.depth)])]
    concatenate x1 -> x0, local copies, waits for them, and re-layouts: 6.77 us -> none  [all_columns(): return jnp.concatenate([first[0], second[0], first[1], second[1]], axis=1)]
    dot_general x5 -> x4, matrix products: 28.8 us -> 23.8 us  [dot_nt(): lax.dot_general(a, b, (((1,), (1,)), ((), ())), preferred_element_type=F32)]
    unnamed x181 -> x124, local copies, waits for them, and re-layouts: 12.6 us -> 17 us
  transfers between devices with their start and end apart: 103 -> 59, of which waited for: 37 -> 26; matrix products, arithmetic and copies ran while one was open for 24% -> 18% of each run, Pallas kernels for 11% -> 8%
where the time goes in v2:
time: 576 us; the launch traced here: 569 us
  Pallas kernels  187 us (32%)
  waiting for transfers between devices  98.7 us (17%)
  starting transfers between devices  95.9 us (17%)
  local copies, waits for them, and re-layouts  94.4 us (16%)
  other arithmetic  46.3 us (8%)
  matrix products  44.5 us (8%)
    pallas_call x1, Pallas kernels, front(): pl.pallas_call(functools.partial(front_kernel, depth, rows, width, in_col...  130 us
    ppermute x59, waiting for transfers between devices, send(): return lax.ppermute(value, ('dp', 'mp'), self.pairs(move))  98.7 us
    ppermute x59, starting transfers between devices, send(): return lax.ppermute(value, ('dp', 'mp'), self.pairs(move))  95.9 us
    dot_general x4, matrix products, dot_nt(): lax.dot_general(a, b, (((1,), (1,)), ((), ())), preferred_element_type=F32)  23.8 us
    pallas_call x3, Pallas kernels, wgrad_plane(): pl.pallas_call(functools.partial(wgrad_plane_kernel, depth, rows, pad), o...  22.8 us
    pallas_call x1, Pallas kernels, attend_back(): pl.pallas_call(functools.partial(attend_back_kernel, tokens), out_shape=[...  21.6 us
    dot_general x4, matrix products, dot(): return jnp.dot(a, b, preferred_element_type=F32)  20.7 us
    unnamed x124, local copies, waits for them, and re-layouts  17 us
  transfers between devices with their start and end apart: 59, of which 26 were waited for; matrix products, arithmetic and copies ran while one was open for 18% of the time, Pallas kernels for 8%

profile of v2, /device:TPU:0, one launch (start us, length us, event | category | flops | bytes accessed | tf_op | source)
XLA Modules:
  0.0 568.7 jit_solution(8330125516176218896)
XLA Ops:
  9.9 130.5 %front.1 = (bf16[512,960]{1,0:T(8,128)(2,1)}, bf16[4,512,640]{2,1,0:T(8,128)(2,1)}, bf16[512,960]{1,0:T(8,128)(2,1)}, f32[16,512]{1,0:T(8,128)}, f32[512,1024]{1...) custom-call(bf16[128,640]{1,0:T(8,128)(2,1)} %pad_maximum_fusion.20., ...), custom_call_target="tpu_custom_call" | custom-call | flops 21474836480 | bytes 41943040 | tf_op jit(solution)/shard_map/front/pallas_call | solution.py:478
  146.0 4.6 fusion.66
  165.4 5.7 fusion.65
  181.9 4.7 fusion.13
  186.7 4.7 fusion.15
  191.4 9.0 %multiply_convert_fusion = (bf16[1024,1280]{1,0:T(8,128)(2,1)}, bf16[1024,1280]{1,0:T(8,128)(2,1)}, bf16[1024,1280]{1,0:T(8,128)(2,1)S(1)}) fusion(f32[1024,1280]{1,0:T(8,128)S(1)} %fusion.15, f32[1024,1280]{1,0:T(8,128)S(1)} %fusion.13, bf16[1024,640]{1,0:T(8,128)(2,1)S(1)} %bitcast.258, bf16[1024,640]{1,0:T(8,128)(2,1)S(1)} %bitcast.256, ...), kind=kOutput, calls=%fused_computation | convolution fusion | flops 2713452544 | bytes 23068672 | tf_op jit(solution)/shard_map/dot_general | solution.py:27
  201.9 4.5 fusion.12
  206.4 4.5 copy.190
  210.9 7.4 %fusion.14 = f32[1024,1024]{0,1:T(8,128)} fusion(bf16[1024,1280]{1,0:T(8,128)(2,1)} %get-tuple-element.149, bf16[1024,640]{1,0:T(8,128)(2,1)} %bitcast.252, bf16[1024,640]{1,0:T(8,128)(2,1)} %bitcast.254), kind=kOutput, calls=%fused_computation.48 | convolution fusion | flops 2689597440 | bytes 9437184 | tf_op jit(solution)/shard_map/dot_general | solution.py:31
  218.3 4.7 copy.188
  223.0 6.3 %convolution_add_fusion = f32[1024,1024]{0,1:T(8,128)S(1)} fusion(f32[1024,1024]{0,1:T(8,128)} %fusion.14, bf16[1024,1280]{1,0:T(8,128)(2,1)} %get-tuple-element.148, bf16[1024,640]{1,0:T(8,128)(2,1)S(1)} %bitcast.249, bf16[1024,640]{1,0:T(8,128)(2,1)} %bitcast.250), kind=kOutput, calls=%fused_computation.44 | convolution fusion | flops 2690646016 | bytes 13631488 | tf_op jit(solution)/shard_map/dot_general | solution.py:31
  240.0 7.4 %wgrad_plane.5 = (bf16[4,120,640]{2,1,0:T(8,128)(2,1)}, bf16[2,120,640]{2,1,0:T(8,128)(2,1)}, bf16[2,120,640]{2,1,0:T(8,128)(2,1)}, bf16[2,120,640]{2,1,0:T(8,12...) custom-call(s32[3]{0:T(128)} %pad_add_fusion.ids, ...), custom_call_target="tpu_custom_call" | custom-call | flops 2684354560 | bytes 7340032 | tf_op jit(solution)/shard_map/wgrad_plane/pallas_call | solution.py:134
  250.0 4.4 copy.189
  257.6 7.4 %wgrad_plane.4 = (bf16[4,120,640]{2,1,0:T(8,128)(2,1)}, bf16[2,120,640]{2,1,0:T(8,128)(2,1)}, bf16[2,120,640]{2,1,0:T(8,128)(2,1)}, bf16[2,120,640]{2,1,0:T(8,12...) custom-call(s32[3]{0:T(128)} %pad_add_fusion.ids, ...), custom_call_target="tpu_custom_call" | custom-call | flops 2684354560 | bytes 7340032 | tf_op jit(solution)/shard_map/wgrad_plane/pallas_call | solution.py:134
  265.0 4.5 copy.186
  273.9 7.9 %wgrad_plane.3 = (bf16[4,120,640]{2,1,0:T(8,128)(2,1)}, bf16[2,120,640]{2,1,0:T(8,128)(2,1)}, bf16[2,120,640]{2,1,0:T(8,128)(2,1)}, bf16[2,120,640]{2,1,0:T(8,12...) custom-call(s32[3]{0:T(128)} %pad_add_fusion.ids, ...), custom_call_target="tpu_custom_call" | custom-call | flops 2684354560 | bytes 7340032 | tf_op jit(solution)/shard_map/wgrad_plane/pallas_call | solution.py:134
  286.5 11.8 %collective-permute-done.37 = bf16[2,120,640]{2,1,0:T(8,128)(2,1)S(1)} collective-permute-done((bf16[2,120,640]{2,1,0:T(8,128)(2,1)}, bf16[2,120,640]{2,1,0:T(8,128)(2,1)S(1)}, u32[]{:S(2)}, u32[]{:S(2)}) %collective-permute-start.37) | collective-permute-done | bytes 307232 | tf_op jit(solution)/shard_map/ppermute | solution.py:57
  300.6 5.7 %collective-permute-done.28 = bf16[2,120,640]{2,1,0:T(8,128)(2,1)S(1)} collective-permute-done((bf16[2,120,640]{2,1,0:T(8,128)(2,1)S(1)}, bf16[2,120,640]{2,1,0:T(8,128)(2,1)S(1)}, u32[]{:S(2)}, u32[]{:S(2)}) %collective-permute-start.28) | collective-permute-done | bytes 307232 | tf_op jit(solution)/shard_map/ppermute | solution.py:57
  318.9 6.3 %collective-permute-done.36 = bf16[2,120,640]{2,1,0:T(8,128)(2,1)S(1)} collective-permute-done((bf16[2,120,640]{2,1,0:T(8,128)(2,1)S(1)}, bf16[2,120,640]{2,1,0:T(8,128)(2,1)S(1)}, u32[]{:S(2)}, u32[]{:S(2)}) %collective-permute-start.36) | collective-permute-done | bytes 307232 | tf_op jit(solution)/shard_map/ppermute | solution.py:57
  328.7 5.8 %collective-permute-done.41 = bf16[2,120,640]{2,1,0:T(8,128)(2,1)S(1)} collective-permute-done((bf16[2,120,640]{2,1,0:T(8,128)(2,1)S(1)}, bf16[2,120,640]{2,1,0:T(8,128)(2,1)S(1)}, u32[]{:S(2)}, u32[]{:S(2)}) %collective-permute-start.41) | collective-permute-done | bytes 307232 | tf_op jit(solution)/shard_map/ppermute | solution.py:57
  342.3 5.8 %collective-permute-start.53 = (bf16[120,640]{1,0:T(8,128)(2,1)S(1)}, bf16[120,640]{1,0:T(8,128)(2,1)S(1)}, u32[]{:S(2)}, u32[]{:S(2)}) collective-permute-start(bf16[120,640]{1,0:T(8,128)(2,1)S(1)} %get-tuple-element.181), channel_id=1, source_target_pairs={{0,24},{1,25},{2,26},{3,27},{4,28},{5,29},{6,30},{7,31},{8,16},{9,... | collective-permute-start | bytes 460808 | tf_op jit(solution)/shard_map/ppermute | solution.py:57
  348.5 10.5 %collective-permute-done.52 = bf16[120,640]{1,0:T(8,128)(2,1)S(1)} collective-permute-done((bf16[120,640]{1,0:T(8,128)(2,1)S(1)}, bf16[120,640]{1,0:T(8,128)(2,1)S(1)}, u32[]{:S(2)}, u32[]{:S(2)}) %collective-permute-start.52) | collective-permute-done | bytes 153632 | tf_op jit(solution)/shard_map/ppermute | solution.py:57
  360.9 9.4 %collective-permute-start.33 = (bf16[120,640]{1,0:T(8,128)(2,1)S(1)}, bf16[120,640]{1,0:T(8,128)(2,1)S(1)}, u32[]{:S(2)}, u32[]{:S(2)}) collective-permute-start(bf16[120,640]{1,0:T(8,128)(2,1)S(1)} %get-tuple-element.186), channel_id=1, source_target_pairs={{0,8},{1,9},{2,10},{3,11},{4,12},{5,13},{6,14},{7,15},{8,0},{9,1},... | collective-permute-start | bytes 460808 | tf_op jit(solution)/shard_map/ppermute | solution.py:57
  375.1 6.2 %collective-permute-done.34 = bf16[120,640]{1,0:T(8,128)(2,1)S(1)} collective-permute-done((bf16[120,640]{1,0:T(8,128)(2,1)S(1)}, bf16[120,640]{1,0:T(8,128)(2,1)S(1)}, u32[]{:S(2)}, u32[]{:S(2)}) %collective-permute-start.34) | collective-permute-done | bytes 153632 | tf_op jit(solution)/shard_map/ppermute | solution.py:57
  396.3 4.8 wgrad_all.3
  401.1 21.6 %attend_back.1 = (f32[512,960]{1,0:T(8,128)}, bf16[512,640]{1,0:T(8,128)(2,1)}, bf16[512,640]{1,0:T(8,128)(2,1)}, f32[512,640]{1,0:T(8,128)}) custom-call(s32[2]{0:T(128)} %and_select_fusion.first, s32[1,512]{1,0:T(1,128)} %broadcast_subtract_fusion.seg, bf16[512,960]{1,0:T(8,128)(2,1)} %get-tuple-element.52.q, bf16[512,640]{1,0:T(8,128)(2,1)} %get-tuple-element.165.kv2, ...), custom_call_target="tpu_custom_call" | custom-call | flops 34359738368 | bytes 10485760 | tf_op jit(solution)/shard_map/attend_back/pallas_call | solution.py:579
  428.5 10.4 %collective-permute-start.19 = (bf16[2,120,240]{2,1,0:T(8,128)(2,1)}, bf16[2,120,240]{2,1,0:T(8,128)(2,1)}, u32[]{:S(2)}, u32[]{:S(2)}) collective-permute-start(bf16[2,120,240]{2,1,0:T(8,128)(2,1)} %get-tuple-element.177), channel_id=1, source_target_pairs={{0,2},{1,3},{2,0},{3,1},{4,6},{5,7},{6,4},{7,5},{8,10},{9,11},{10,... | collective-permute-start | bytes 345608 | tf_op jit(solution)/shard_map/ppermute | solution.py:57
  438.9 9.1 %collective-permute-start.22 = (bf16[2,120,240]{2,1,0:T(8,128)(2,1)S(1)}, bf16[2,120,240]{2,1,0:T(8,128)(2,1)}, u32[]{:S(2)}, u32[]{:S(2)}) collective-permute-start(bf16[2,120,240]{2,1,0:T(8,128)(2,1)S(1)} %get-tuple-element.175), channel_id=1, source_target_pairs={{0,4},{1,5},{2,6},{3,7},{4,0},{5,1},{6,2},{7,3},{8,12},{9,13},{10,... | collective-permute-start | bytes 345608 | tf_op jit(solution)/shard_map/ppermute | solution.py:57
  463.3 14.6 %collective-permute-done.23 = bf16[2,120,240]{2,1,0:T(8,128)(2,1)S(1)} collective-permute-done((bf16[2,120,240]{2,1,0:T(8,128)(2,1)S(1)}, bf16[2,120,240]{2,1,0:T(8,128)(2,1)S(1)}, u32[]{:S(2)}, u32[]{:S(2)}) %collective-permute-start.23) | collective-permute-done | bytes 115232 | tf_op jit(solution)/shard_map/ppermute | solution.py:57
  491.5 7.1 %wgrad_all.2 = (bf16[2,2,4,120,400]{4,3,2,1,0:T(8,128)(2,1)}, bf16[2,2,4,120,400]{4,3,2,1,0:T(8,128)(2,1)}) custom-call(s32[3]{0:T(128)} %pad_add_fusion.ids, bf16[1024,512]{1,0:T(8,128)(2,1)} %bitcast.261, bf16[4,512,400]{2,1,0:T(8,128)(2,1)} %bitcast.246), custom_call_target="tpu_custom_call" | custom-call | flops 1677721600 | bytes 7602176 | tf_op jit(solution)/shard_map/wgrad_all/pallas_call | solution.py:171
  502.8 5.5 fusion.8
  512.6 6.0 %collective-permute-start.25 = (bf16[120,240]{1,0:T(8,128)(2,1)S(1)}, bf16[120,240]{1,0:T(8,128)(2,1)S(1)}, u32[]{:S(2)}, u32[]{:S(2)}) collective-permute-start(bf16[120,240]{1,0:T(8,128)(2,1)S(1)} %get-tuple-element.194), channel_id=1, source_target_pairs={{0,16},{1,17},{2,18},{3,19},{4,20},{5,21},{6,22},{7,23},{8,24},{9,... | collective-permute-start | bytes 172808 | tf_op jit(solution)/shard_map/ppermute | solution.py:57
  (344 shorter events, 207.9 us)
Async XLA Ops:
  142.8 39.1 %collective-permute-start = (bf16[512,1024]{0,1:T(8,128)(2,1)}, bf16[512,1024]{0,1:T(8,128)(2,1)}, u32[]{:S(2)}, u32[]{:S(2)}) collective-permute-start(bf16[512,1024]{0,1:T(8,128)(2,1)} %copy.163), channel_id=1, source_target_pairs={{0,1},{1,0},{2,3},{3,2},{4,5},{5,4},{6,7},{7,6},{8,9},{9,8},{10,11... | collective-permute-start | bytes 3145736 | tf_op jit(solution)/shard_map/ppermute | solution.py:57
  144.0 47.4 %collective-permute-start.2 = (bf16[512,1024]{0,1:T(8,128)(2,1)}, bf16[512,1024]{0,1:T(8,128)(2,1)}, u32[]{:S(2)}, u32[]{:S(2)}) collective-permute-start(bf16[512,1024]{0,1:T(8,128)(2,1)} %bitcast.26), channel_id=1, source_target_pairs={{0,1},{1,0},{2,3},{3,2},{4,5},{5,4},{6,7},{7,6},{8,9},{9,8},{10,11... | collective-permute-start | bytes 3145736 | tf_op jit(solution)/shard_map/ppermute | solution.py:57
  232.5 150.2 %collective-permute-start.3 = (bf16[512,1024]{0,1:T(8,128)(2,1)}, bf16[512,1024]{0,1:T(8,128)(2,1)}, u32[]{:S(2)}, u32[]{:S(2)}) collective-permute-start(bf16[512,1024]{0,1:T(8,128)(2,1)} %slice.414), channel_id=1, source_target_pairs={{0,1},{1,0},{2,3},{3,2},{4,5},{5,4},{6,7},{7,6},{8,9},{9,8},{10,11... | collective-permute-start | bytes 3145736 | tf_op jit(solution)/shard_map/ppermute | solution.py:57
  247.4 36.9 %collective-permute-start.46 = (bf16[2,120,640]{2,1,0:T(8,128)(2,1)}, bf16[2,120,640]{2,1,0:T(8,128)(2,1)S(1)}, u32[]{:S(2)}, u32[]{:S(2)}) collective-permute-start(bf16[2,120,640]{2,1,0:T(8,128)(2,1)} %get-tuple-element.83), channel_id=1, source_target_pairs={{0,2},{1,3},{2,0},{3,1},{4,6},{5,7},{6,4},{7,5},{8,10},{9,11},{10,... | collective-permute-start | bytes 921608 | tf_op jit(solution)/shard_map/ppermute | solution.py:57
  248.0 37.0 %collective-permute-start.49 = (bf16[2,120,640]{2,1,0:T(8,128)(2,1)}, bf16[2,120,640]{2,1,0:T(8,128)(2,1)S(1)}, u32[]{:S(2)}, u32[]{:S(2)}) collective-permute-start(bf16[2,120,640]{2,1,0:T(8,128)(2,1)} %get-tuple-element.86), channel_id=1, source_target_pairs={{0,4},{1,5},{2,6},{3,7},{4,0},{5,1},{6,2},{7,3},{8,12},{9,13},{10,... | collective-permute-start | bytes 921608 | tf_op jit(solution)/shard_map/ppermute | solution.py:57
  249.4 65.4 %collective-permute-start.48 = (bf16[2,120,640]{2,1,0:T(8,128)(2,1)}, bf16[2,120,640]{2,1,0:T(8,128)(2,1)S(1)}, u32[]{:S(2)}, u32[]{:S(2)}) collective-permute-start(bf16[2,120,640]{2,1,0:T(8,128)(2,1)} %get-tuple-element.84), channel_id=1, source_target_pairs={{0,4},{1,5},{2,6},{3,7},{4,0},{5,1},{6,2},{7,3},{8,12},{9,13},{10,... | collective-permute-start | bytes 921608 | tf_op jit(solution)/shard_map/ppermute | solution.py:57
  282.8 25.7 %collective-permute-start.45 = (bf16[2,120,640]{2,1,0:T(8,128)(2,1)S(1)}, bf16[2,120,640]{2,1,0:T(8,128)(2,1)S(1)}, u32[]{:S(2)}, u32[]{:S(2)}) collective-permute-start(bf16[2,120,640]{2,1,0:T(8,128)(2,1)S(1)} %copy-done.54), channel_id=1, source_target_pairs={{0,2},{1,3},{2,0},{3,1},{4,6},{5,7},{6,4},{7,5},{8,10},{9,11},{10,... | collective-permute-start | bytes 921608 | tf_op jit(solution)/shard_map/ppermute | solution.py:57
  284.3 14.0 %collective-permute-start.37 = (bf16[2,120,640]{2,1,0:T(8,128)(2,1)}, bf16[2,120,640]{2,1,0:T(8,128)(2,1)S(1)}, u32[]{:S(2)}, u32[]{:S(2)}) collective-permute-start(bf16[2,120,640]{2,1,0:T(8,128)(2,1)} %get-tuple-element.76), channel_id=1, source_target_pairs={{0,2},{1,3},{2,0},{3,1},{4,6},{5,7},{6,4},{7,5},{8,10},{9,11},{10,... | collective-permute-start | bytes 921608 | tf_op jit(solution)/shard_map/ppermute | solution.py:57
  285.0 14.8 %collective-permute-start.40 = (bf16[2,120,640]{2,1,0:T(8,128)(2,1)S(1)}, bf16[2,120,640]{2,1,0:T(8,128)(2,1)S(1)}, u32[]{:S(2)}, u32[]{:S(2)}) collective-permute-start(bf16[2,120,640]{2,1,0:T(8,128)(2,1)S(1)} %copy-done.56), channel_id=1, source_target_pairs={{0,4},{1,5},{2,6},{3,7},{4,0},{5,1},{6,2},{7,3},{8,12},{9,13},{10,... | collective-permute-start | bytes 921608 | tf_op jit(solution)/shard_map/ppermute | solution.py:57
  308.4 10.2 %collective-permute-start.50 = (bf16[2,120,640]{2,1,0:T(8,128)(2,1)S(1)}, bf16[2,120,640]{2,1,0:T(8,128)(2,1)S(1)}, u32[]{:S(2)}, u32[]{:S(2)}) collective-permute-start(bf16[2,120,640]{2,1,0:T(8,128)(2,1)S(1)} %add_convert_fusion.3), channel_id=1, source_target_pairs={{0,2},{1,3},{2,0},{3,1},{4,6},{5,7},{6,4},{7,5},{8,10},{9,11},{10,... | collective-permute-start | bytes 921608 | tf_op jit(solution)/shard_map/ppermute | solution.py:57
  308.5 16.7 %collective-permute-start.36 = (bf16[2,120,640]{2,1,0:T(8,128)(2,1)S(1)}, bf16[2,120,640]{2,1,0:T(8,128)(2,1)S(1)}, u32[]{:S(2)}, u32[]{:S(2)}) collective-permute-start(bf16[2,120,640]{2,1,0:T(8,128)(2,1)S(1)} %copy-done.53), channel_id=1, source_target_pairs={{0,2},{1,3},{2,0},{3,1},{4,6},{5,7},{6,4},{7,5},{8,10},{9,11},{10,... | collective-permute-start | bytes 921608 | tf_op jit(solution)/shard_map/ppermute | solution.py:57
  314.2 14.4 %collective-permute-start.39 = (bf16[2,120,640]{2,1,0:T(8,128)(2,1)S(1)}, bf16[2,120,640]{2,1,0:T(8,128)(2,1)S(1)}, u32[]{:S(2)}, u32[]{:S(2)}) collective-permute-start(bf16[2,120,640]{2,1,0:T(8,128)(2,1)S(1)} %copy-done.52), channel_id=1, source_target_pairs={{0,4},{1,5},{2,6},{3,7},{4,0},{5,1},{6,2},{7,3},{8,12},{9,13},{10,... | collective-permute-start | bytes 921608 | tf_op jit(solution)/shard_map/ppermute | solution.py:57
  314.8 20.3 %collective-permute-start.27 = (bf16[2,120,640]{2,1,0:T(8,128)(2,1)S(1)}, bf16[2,120,640]{2,1,0:T(8,128)(2,1)S(1)}, u32[]{:S(2)}, u32[]{:S(2)}) collective-permute-start(bf16[2,120,640]{2,1,0:T(8,128)(2,1)S(1)} %copy-done.51), channel_id=1, source_target_pairs={{0,2},{1,3},{2,0},{3,1},{4,6},{5,7},{6,4},{7,5},{8,10},{9,11},{10,... | collective-permute-start | bytes 921608 | tf_op jit(solution)/shard_map/ppermute | solution.py:57
  328.6 53.5 %collective-permute-start.1 = (bf16[512,1024]{1,0:T(8,128)(2,1)S(1)}, bf16[512,1024]{1,0:T(8,128)(2,1)S(1)}, u32[]{:S(2)}, u32[]{:S(2)}) collective-permute-start(bf16[512,1024]{1,0:T(8,128)(2,1)S(1)} %slice.415), channel_id=1, source_target_pairs={{0,1},{1,0},{2,3},{3,2},{4,5},{5,4},{6,7},{7,6},{8,9},{9,8},{10,11... | collective-permute-start | bytes 3145736 | tf_op jit(solution)/shard_map/ppermute | solution.py:57
  337.1 11.3 %collective-permute-start.51 = (bf16[120,640]{1,0:T(8,128)(2,1)S(1)}, bf16[120,640]{1,0:T(8,128)(2,1)S(1)}, u32[]{:S(2)}, u32[]{:S(2)}) collective-permute-start(bf16[120,640]{1,0:T(8,128)(2,1)S(1)} %get-tuple-element.180), channel_id=1, source_target_pairs={{0,8},{1,9},{2,10},{3,11},{4,12},{5,13},{6,14},{7,15},{8,0},{9,1},... | collective-permute-start | bytes 460808 | tf_op jit(solution)/shard_map/ppermute | solution.py:57
  341.6 17.4 %collective-permute-start.52 = (bf16[120,640]{1,0:T(8,128)(2,1)S(1)}, bf16[120,640]{1,0:T(8,128)(2,1)S(1)}, u32[]{:S(2)}, u32[]{:S(2)}) collective-permute-start(bf16[120,640]{1,0:T(8,128)(2,1)S(1)} %get-tuple-element.182), channel_id=1, source_target_pairs={{0,16},{1,17},{2,18},{3,19},{4,20},{5,21},{6,22},{7,23},{8,24},{9,... | collective-permute-start | bytes 460808 | tf_op jit(solution)/shard_map/ppermute | solution.py:57
  342.3 16.8 %collective-permute-start.53 = (bf16[120,640]{1,0:T(8,128)(2,1)S(1)}, bf16[120,640]{1,0:T(8,128)(2,1)S(1)}, u32[]{:S(2)}, u32[]{:S(2)}) collective-permute-start(bf16[120,640]{1,0:T(8,128)(2,1)S(1)} %get-tuple-element.181), channel_id=1, source_target_pairs={{0,24},{1,25},{2,26},{3,27},{4,28},{5,29},{6,30},{7,31},{8,16},{9,... | collective-permute-start | bytes 460808 | tf_op jit(solution)/shard_map/ppermute | solution.py:57
  348.4 12.4 %collective-permute-start.42 = (bf16[120,640]{1,0:T(8,128)(2,1)S(1)}, bf16[120,640]{1,0:T(8,128)(2,1)S(1)}, u32[]{:S(2)}, u32[]{:S(2)}) collective-permute-start(bf16[120,640]{1,0:T(8,128)(2,1)S(1)} %get-tuple-element.183), channel_id=1, source_target_pairs={{0,8},{1,9},{2,10},{3,11},{4,12},{5,13},{6,14},{7,15},{8,0},{9,1},... | collective-permute-start | bytes 460808 | tf_op jit(solution)/shard_map/ppermute | solution.py:57
  359.1 13.1 %collective-permute-start.43 = (bf16[120,640]{1,0:T(8,128)(2,1)S(1)}, bf16[120,640]{1,0:T(8,128)(2,1)S(1)}, u32[]{:S(2)}, u32[]{:S(2)}) collective-permute-start(bf16[120,640]{1,0:T(8,128)(2,1)S(1)} %get-tuple-element.185), channel_id=1, source_target_pairs={{0,16},{1,17},{2,18},{3,19},{4,20},{5,21},{6,22},{7,23},{8,24},{9,... | collective-permute-start | bytes 460808 | tf_op jit(solution)/shard_map/ppermute | solution.py:57
  359.1 13.1 %collective-permute-start.44 = (bf16[120,640]{1,0:T(8,128)(2,1)S(1)}, bf16[120,640]{1,0:T(8,128)(2,1)S(1)}, u32[]{:S(2)}, u32[]{:S(2)}) collective-permute-start(bf16[120,640]{1,0:T(8,128)(2,1)S(1)} %get-tuple-element.184), channel_id=1, source_target_pairs={{0,24},{1,25},{2,26},{3,27},{4,28},{5,29},{6,30},{7,31},{8,16},{9,... | collective-permute-start | bytes 460808 | tf_op jit(solution)/shard_map/ppermute | solution.py:57
  360.9 14.2 %collective-permute-start.33 = (bf16[120,640]{1,0:T(8,128)(2,1)S(1)}, bf16[120,640]{1,0:T(8,128)(2,1)S(1)}, u32[]{:S(2)}, u32[]{:S(2)}) collective-permute-start(bf16[120,640]{1,0:T(8,128)(2,1)S(1)} %get-tuple-element.186), channel_id=1, source_target_pairs={{0,8},{1,9},{2,10},{3,11},{4,12},{5,13},{6,14},{7,15},{8,0},{9,1},... | collective-permute-start | bytes 460808 | tf_op jit(solution)/shard_map/ppermute | solution.py:57
  401.1 25.3 %collective-permute-start.17 = (bf16[2,2,4,120,240]{4,3,2,1,0:T(8,128)(2,1)}, bf16[2,2,4,120,240]{4,3,2,1,0:T(8,128)(2,1)}, u32[]{:S(2)}, u32[]{:S(2)}) collective-permute-start(bf16[2,2,4,120,240]{4,3,2,1,0:T(8,128)(2,1)} %get-tuple-element.65), channel_id=1, source_target_pairs={{0,1},{1,0},{2,3},{3,2},{4,5},{5,4},{6,7},{7,6},{8,9},{9,8},{10,11... | collective-permute-start | bytes 2764808 | tf_op jit(solution)/shard_map/ppermute | solution.py:57
  422.7 32.0 %collective-permute-start.5 = (bf16[512,640]{1,0:T(8,128)(2,1)}, bf16[512,640]{1,0:T(8,128)(2,1)}, u32[]{:S(2)}, u32[]{:S(2)}) collective-permute-start(bf16[512,640]{1,0:T(8,128)(2,1)} %get-tuple-element.59), channel_id=1, source_target_pairs={{2,3},{6,7},{10,11},{14,15},{18,19},{22,23},{26,27},{30,31}} | collective-permute-start | bytes 1966088 | tf_op jit(solution)/shard_map/ppermute | solution.py:57
  424.3 54.6 %collective-permute-start.4 = (bf16[512,640]{1,0:T(8,128)(2,1)}, bf16[512,640]{1,0:T(8,128)(2,1)}, u32[]{:S(2)}, u32[]{:S(2)}) collective-permute-start(bf16[512,640]{1,0:T(8,128)(2,1)} %get-tuple-element.59), channel_id=1, source_target_pairs={{1,0},{3,2},{5,4},{7,6},{9,8},{11,10},{13,12},{15,14},{17,16},{19,... | collective-permute-start | bytes 1966088 | tf_op jit(solution)/shard_map/ppermute | solution.py:57
  428.5 21.6 %collective-permute-start.19 = (bf16[2,120,240]{2,1,0:T(8,128)(2,1)}, bf16[2,120,240]{2,1,0:T(8,128)(2,1)}, u32[]{:S(2)}, u32[]{:S(2)}) collective-permute-start(bf16[2,120,240]{2,1,0:T(8,128)(2,1)} %get-tuple-element.177), channel_id=1, source_target_pairs={{0,2},{1,3},{2,0},{3,1},{4,6},{5,7},{6,4},{7,5},{8,10},{9,11},{10,... | collective-permute-start | bytes 345608 | tf_op jit(solution)/shard_map/ppermute | solution.py:57
  438.9 12.4 %collective-permute-start.22 = (bf16[2,120,240]{2,1,0:T(8,128)(2,1)S(1)}, bf16[2,120,240]{2,1,0:T(8,128)(2,1)}, u32[]{:S(2)}, u32[]{:S(2)}) collective-permute-start(bf16[2,120,240]{2,1,0:T(8,128)(2,1)S(1)} %get-tuple-element.175), channel_id=1, source_target_pairs={{0,4},{1,5},{2,6},{3,7},{4,0},{5,1},{6,2},{7,3},{8,12},{9,13},{10,... | collective-permute-start | bytes 345608 | tf_op jit(solution)/shard_map/ppermute | solution.py:57
  456.3 22.6 %collective-permute-start.6 = (bf16[512,640]{1,0:T(8,128)(2,1)S(1)}, bf16[512,640]{1,0:T(8,128)(2,1)S(1)}, u32[]{:S(2)}, u32[]{:S(2)}) collective-permute-start(bf16[512,640]{1,0:T(8,128)(2,1)S(1)} %add_convert_fusion.2), channel_id=1, source_target_pairs={{2,0},{3,1},{6,4},{7,5},{10,8},{11,9},{14,12},{15,13},{18,16},{19,... | collective-permute-start | bytes 1966088 | tf_op jit(solution)/shard_map/ppermute | solution.py:57
  457.7 20.2 %collective-permute-start.23 = (bf16[2,120,240]{2,1,0:T(8,128)(2,1)S(1)}, bf16[2,120,240]{2,1,0:T(8,128)(2,1)S(1)}, u32[]{:S(2)}, u32[]{:S(2)}) collective-permute-start(bf16[2,120,240]{2,1,0:T(8,128)(2,1)S(1)} %get-tuple-element.179), channel_id=1, source_target_pairs={{0,2},{1,3},{2,0},{3,1},{4,6},{5,7},{6,4},{7,5},{8,10},{9,11},{10,... | collective-permute-start | bytes 345608 | tf_op jit(solution)/shard_map/ppermute | solution.py:57
  502.8 28.7 %collective-permute-start.7 = (bf16[2,2,4,120,400]{3,4,2,1,0:T(8,128)(2,1)}, bf16[2,2,4,120,400]{3,4,2,1,0:T(8,128)(2,1)}, u32[]{:S(2)}, u32[]{:S(2)}) collective-permute-start(bf16[2,2,4,120,400]{3,4,2,1,0:T(8,128)(2,1)} %copy.182), channel_id=1, source_target_pairs={{0,1},{1,0},{2,3},{3,2},{4,5},{5,4},{6,7},{7,6},{8,9},{9,8},{10,11... | collective-permute-start | bytes 4608008 | tf_op jit(solution)/shard_map/ppermute | solution.py:57
  508.3 11.6 %collective-permute-start.54 = (f32[2,1024]{1,0:T(2,128)S(1)}, f32[2,1024]{1,0:T(2,128)S(1)}, u32[]{:S(2)}, u32[]{:S(2)}) collective-permute-start(f32[2,1024]{1,0:T(2,128)S(1)} %pad_maximum_fusion.22), channel_id=1, source_target_pairs={{0,1},{1,0},{2,3},{3,2},{4,5},{5,4},{6,7},{7,6},{8,9},{9,8},{10,11... | collective-permute-start | bytes 24584 | tf_op jit(solution)/shard_map/ppermute | solution.py:57
  508.9 11.1 %collective-permute-start.24 = (bf16[120,240]{1,0:T(8,128)(2,1)S(1)}, bf16[120,240]{1,0:T(8,128)(2,1)S(1)}, u32[]{:S(2)}, u32[]{:S(2)}) collective-permute-start(bf16[120,240]{1,0:T(8,128)(2,1)S(1)} %get-tuple-element.192), channel_id=1, source_target_pairs={{0,8},{1,9},{2,10},{3,11},{4,12},{5,13},{6,14},{7,15},{8,0},{9,1},... | collective-permute-start | bytes 172808 | tf_op jit(solution)/shard_map/ppermute | solution.py:57
  540.9 10.1 %collective-permute-start.8 = (bf16[2,120,400]{2,1,0:T(8,128)(2,1)S(1)}, bf16[2,120,400]{2,1,0:T(8,128)(2,1)S(1)}, u32[]{:S(2)}, u32[]{:S(2)}) collective-permute-start(bf16[2,120,400]{2,1,0:T(8,128)(2,1)S(1)} %get-tuple-element.168), channel_id=1, source_target_pairs={{0,2},{1,3},{2,0},{3,1},{4,6},{5,7},{6,4},{7,5},{8,10},{9,11},{10,... | collective-permute-start | bytes 576008 | tf_op jit(solution)/shard_map/ppermute | solution.py:57
  (85 other events, 644.8 us)
